TPU v7x, 128 devices: a whole 4x4x4 slice. The times are simulated.
128 devices in a mesh: slab: 16 (over x, z_hi, core), xy: 8 (over z_lo, y).
Axes of the slice: x: 4, y: 4, z: 4 (z_hi: 2, z_lo: 2; z = z_hi * 2 + z_lo), core: 2. Of those that a mesh axis runs over, the one named last changes fastest.
Arguments:
- volume: float32 [32, 64, 512], P('slab', 'xy'), may hold values from 0 to 1
- footprint: bfloat16 [32, 64, 4, 2, 128, 256], P('slab', 'xy'), may hold values from 0.049804688 to 1
- tile_block: int32 [32, 64, 4, 2], P('slab', 'xy'), may hold values from 0 to 511, as said below
- tile_cells: int32 [32, 64, 4, 2], P('slab', 'xy'), may hold values from 1 to 256, as said below
- measured: float32 [2, 131072], replicated, may hold values from 0 to 512
Outputs:
- updated: float32 [32, 64, 512], P('slab', 'xy')
- correction: float32 [2, 131072], P(None, ('slab', 'xy'))
Inputs may be any that keep to these rules, and one draw needn't show every extreme that they name: `tile_cells`: at least one tile of some view has all 256 cells live. `tile_block`: A tile's block lies in detector row about plane * 2, off by at most one below and 2 above (within the detector); its column block follows the tile's place along the row for even views and the row's place in the plane for odd views, off by at most one.
All inputs are finite; a program needn't handle non-finite values.
Results may differ from a plain program's by a relative error of at most 0.0003.
Values may be sent and summed in bfloat16 or wider, within the bound.
A program may use at most 64 MiB of HBM per device.

v0:
```python
import jax
import jax.numpy as jnp
from jax import lax
from jax.sharding import PartitionSpec as P

RELAX = 1.0
TV_RATE = 0.8
SMOOTHING = 0.01


def extended(cells, sides, width):
    for axis, dim in sides:
        count = lax.axis_size(axis)
        ends = count - 1
        head = lax.slice_in_dim(cells, 0, width, axis=dim)
        tail = lax.slice_in_dim(cells, cells.shape[dim] - width, cells.shape[dim], axis=dim)
        cells = jnp.concatenate(
            [
                lax.ppermute(tail, axis, [(i, (i + 1) % count) for i in range(ends)]),
                cells,
                lax.ppermute(head, axis, [((i + 1) % count, i) for i in range(ends)]),
            ],
            axis=dim,
        )
    return cells


def tv_slope(padded):
    base = padded[:-1, :-1, :-1]
    diff_a = padded[1:, :-1, :-1] - base
    diff_b = padded[:-1, 1:, :-1] - base
    diff_e = padded[:-1, :-1, 1:] - base
    size = jnp.sqrt(diff_a * diff_a + diff_b * diff_b + diff_e * diff_e + SMOOTHING)
    unit_a = diff_a / size
    unit_b = diff_b / size
    unit_e = diff_e / size
    total = unit_a + unit_b + unit_e
    return -total[1:, 1:, 1:] + unit_a[:-1, 1:, 1:] + unit_b[1:, :-1, 1:] + unit_e[1:, 1:, :-1]


def slope_scale(slope):
    return jnp.sqrt(lax.psum(jnp.sum(slope * slope), ("slab", "xy")) + 1e-06)


def body(volume, footprint, tile_block, tile_cells, measured):
    planes, rows, ycells = volume.shape
    views, tvox, tdet = (footprint.shape[3], footprint.shape[4], footprint.shape[5])
    count = planes * rows * footprint.shape[2]
    detector = measured.shape[1]
    nblocks = detector // tdet
    weights = footprint.reshape(count, views, tvox, tdet)
    block_of = tile_block.reshape(count, views)
    lane = jnp.arange(tdet, dtype=jnp.int32)
    live = lane[None, None, :] < tile_cells.reshape(count, views)[:, :, None]
    masked = jnp.where(live[:, :, None, :], weights, jnp.zeros((), jnp.bfloat16))
    voxels = volume.astype(jnp.bfloat16).reshape(count, tvox)
    contrib = jnp.einsum("tj,tvjc->tvc", voxels, masked, preferred_element_type=jnp.float32)
    rays = jnp.sum(masked, axis=2, dtype=jnp.float32)
    onehot = (block_of[:, :, None] == jnp.arange(nblocks, dtype=jnp.int32)).astype(jnp.float32)
    projected = jnp.einsum(
        "tvn,tvc->vnc", onehot, contrib, precision=lax.Precision.HIGHEST
    ).reshape(views, detector)
    ray_weight = jnp.einsum("tvn,tvc->vnc", onehot, rays, precision=lax.Precision.HIGHEST).reshape(
        views, detector
    )
    share = detector // (lax.axis_size("slab") * lax.axis_size("xy"))
    position = lax.axis_index(("slab", "xy")) * share
    projected, ray_weight = lax.psum((projected, ray_weight), ("slab", "xy"))
    correction_all = (measured - projected) / jnp.maximum(ray_weight, 1.0)
    correction = lax.dynamic_slice_in_dim(correction_all, position, share, 1)
    correction_b = correction_all.astype(jnp.bfloat16)
    blocked = correction_b.reshape(views, nblocks, tdet)
    picked = blocked[jnp.arange(views, dtype=jnp.int32)[None, :], block_of]
    back = jnp.einsum("tvjc,tvc->tj", masked, picked, preferred_element_type=jnp.float32)
    column = jnp.sum(masked, axis=(1, 3), dtype=jnp.float32)
    shift = (back / column).reshape(planes, rows, ycells)
    sart = jnp.maximum(volume + RELAX * shift, 0.0)
    step_gap = sart - volume
    update_norm = jnp.sqrt(lax.psum(jnp.sum(step_gap * step_gap), ("slab", "xy")))
    current = sart
    for turn in range(2):
        rimmed = extended(current, (("slab", 0), ("xy", 1)), 1)
        padded = jnp.pad(rimmed, ((0, 0), (0, 0), (1, 1)))
        slope = tv_slope(padded)
        current = current - TV_RATE * update_norm / slope_scale(slope) * slope
    return (current, correction)


def solution(mesh):
    placed = (
        P("slab", "xy", None),
        P("slab", "xy", None, None, None, None),
        P("slab", "xy", None, None),
        P("slab", "xy", None, None),
        P(),
    )
    return jax.shard_map(
        body,
        mesh=mesh,
        in_specs=placed,
        out_specs=(P("slab", "xy", None), P(None, ("slab", "xy"))),
        check_vma=False,
    )
```

profile of v0, /device:TPU:1, one launch (start us, length us, event | category | flops | bytes accessed | tf_op | source)
XLA Modules:
  0.0 378.8 jit_solution(218229469274358461)
XLA Ops:
  8.9 0.8 copy.30
  10.0 6.0 %convert_reduce_fusion = (f32[2,8,4,128]{3,2,1,0:T(4,128)S(1)}, f32[2,8,4,2,256]{4,3,2,1,0:T(2,128)S(1)}) fusion(bf16[2,8,4,2,128,256]{5,4,3,2,1,0:T(8,128)(2,1)} %param.6, pred[2,8,4,2,256]{4,3,2,1,0:T(4,128)(4,1)S(1)} %iota_compare_fusion.5), kind=kLoop, calls=%fused_computation.1 | loop fusion | flops 16736256 | bytes 8585216 | tf_op jit(solution)/shard_map/reduce_sum | solution.py:75
  16.7 1.8 copy.33
  18.6 7.3 %bitcast_select_fusion = bf16[64,2,128,256]{3,2,1,0:T(8,128)(2,1)} fusion(bf16[2,8,4,2,128,256]{5,4,3,2,1,0:T(8,128)(2,1)} %param.6, pred[64,2,256]{2,1,0:T(4,128)(4,1)S(1)} %iota_compare_fusion.6), kind=kLoop, calls=%fused_computation.3 | loop fusion | flops 4194304 | bytes 16809984 | tf_op jit(solution)/shard_map/jit(_where)/select_n | solution.py:55
  25.9 4.7 %fusion.20 = f32[64,1,2,256]{3,1,2,0:T(1,128)S(1)} fusion(bf16[64,2,128,256]{3,2,1,0:T(8,128)(2,1)} %bitcast_select_fusion, bf16[64,128,1,1]{1,2,3,0:T(2,128)(2,1)S(1)} %reshape.88), kind=kOutput, calls=%fused_computation.74 | convolution fusion | flops 8388608 | bytes 8536064 | tf_op jit(solution)/shard_map/tj,tvjc->tvc/dot_general | solution.py:57
  31.2 1.8 copy.32
  33.4 154.1 %all-reduce.6.cloned.1.call-done = (f32[2,131072]{1,0:T(2,128)}, f32[2,131072]{1,0:T(2,128)}) async-done(((f32[2,131072]{1,0:T(2,128)}, f32[2,131072]{1,0:T(2,128)}), (f32[2,131072]{1,0:T(2,128)}, f32[2,131072]{1,0:T(2,128)})) %all-reduce.6.cloned.1.call-update) | async-done | bytes 2097168 | tf_op jit(solution)/shard_map/psum | solution.py:68
  187.6 2.6 fusion.17
  190.3 1.1 gather_fusion
  191.4 5.6 %fusion.21 = f32[64,1,128,1]{2,1,3,0:T(1,128)S(1)} fusion(bf16[64,2,128,256]{3,2,1,0:T(8,128)(2,1)} %bitcast_select_fusion, bf16[64,2,256,1]{2,3,1,0:T(2,128)(2,1)S(1)} %reshape.90), kind=kOutput, calls=%fused_computation.75 | convolution fusion | flops 8388608 | bytes 8486912 | tf_op jit(solution)/shard_map/tvjc,tvc->tj/dot_general | solution.py:74
  197.7 4.6 %collective-permute-start = (f32[1,8,512]{2,1,0:T(8,128)S(1)}, f32[1,8,512]{2,1,0:T(8,128)S(1)}, u32[]{:S(2)}, u32[]{:S(2)}) collective-permute-start(f32[1,8,512]{2,1,0:T(8,128)S(1)} %get-tuple-element.30), channel_id=1, source_target_pairs={{0,8},{8,16},{16,24},{24,32},{32,40},{40,48},{48,56},{56,64},{64,7... | collective-permute-start | bytes 49160 | tf_op jit(solution)/shard_map/ppermute | solution.py:19
  202.3 1.9 collective-permute-start.1
  204.3 4.6 %collective-permute-done.1 = f32[1,8,512]{2,1,0:T(8,128)S(1)} collective-permute-done((f32[1,8,512]{2,1,0:T(8,128)S(1)}, f32[1,8,512]{2,1,0:T(8,128)S(1)}, u32[]{:S(2)}, u32[]{:S(2)}) %collective-permute-start.1) | collective-permute-done | bytes 16416 | tf_op jit(solution)/shard_map/ppermute | solution.py:21
  208.9 1.3 collective-permute-start.2
  210.2 1.3 collective-permute-start.3
  211.5 3.1 collective-permute-done.3
  215.8 68.0 %all-reduce.2 = (f32[]{:T(128)}, f32[]{:T(128)}) all-reduce(f32[]{:T(128)} %get-tuple-element.14, f32[]{:T(128)} %get-tuple-element.12), channel_id=1, replica_groups=mesh['slab'=16,'xy'=8] {'slab','xy'}, use_global_device_ids=true, to_apply=%region_5.6 | all-reduce | flops 2 | bytes 16 | tf_op jit(solution)/shard_map/psum | solution.py:79
  285.2 4.9 %collective-permute-start.4 = (f32[1,8,512]{2,1,0:T(8,128)S(1)}, f32[1,8,512]{2,1,0:T(8,128)S(1)}, u32[]{:S(2)}, u32[]{:S(2)}) collective-permute-start(f32[1,8,512]{2,1,0:T(8,128)S(1)} %get-tuple-element.28), channel_id=1, source_target_pairs={{0,8},{8,16},{16,24},{24,32},{32,40},{40,48},{48,56},{56,64},{64,7... | collective-permute-start | bytes 49160 | tf_op jit(solution)/shard_map/ppermute | solution.py:19
  290.1 1.9 collective-permute-start.5
  292.0 4.6 %collective-permute-done.5 = f32[1,8,512]{2,1,0:T(8,128)S(1)} collective-permute-done((f32[1,8,512]{2,1,0:T(8,128)S(1)}, f32[1,8,512]{2,1,0:T(8,128)S(1)}, u32[]{:S(2)}, u32[]{:S(2)}) %collective-permute-start.5) | collective-permute-done | bytes 16416 | tf_op jit(solution)/shard_map/ppermute | solution.py:21
  296.7 1.3 collective-permute-start.6
  298.0 1.3 collective-permute-start.7
  299.9 2.5 collective-permute-done.7
  303.5 67.1 %psum.39 = f32[]{:T(128)} all-reduce(f32[]{:T(128)} %get-tuple-element.8), channel_id=1, replica_groups=mesh['slab'=16,'xy'=8] {'slab','xy'}, use_global_device_ids=true, to_apply=%region_9.10 | all-reduce | flops 1 | bytes 8 | tf_op jit(solution)/shard_map/psum | solution.py:42
  (42 shorter events, 8.0 us)
Async XLA Ops:
  7.2 180.4 %all-reduce.6.cloned.1.call-start = ((), (), s32[]{:S(2)}) async-start(), calls=%async_computation | async-start | bytes 4194304 | tf_op jit(solution)/shard_map/psum | solution.py:68
  25.9 161.7 %copy-start = (f32[2,131072]{1,0:T(2,128)S(1)}, f32[2,131072]{1,0:T(2,128)}, u32[]{:S(2)}) copy-start(f32[2,131072]{1,0:T(2,128)} %param.9) | copy-start | bytes 3145732
  33.1 164.1 %copy-start.1 = (f32[2,8,512]{2,1,0:T(8,128)S(1)}, f32[2,8,512]{2,1,0:T(8,128)}, u32[]{:S(2)}) copy-start(f32[2,8,512]{2,1,0:T(8,128)} %param.5) | copy-start | bytes 98308
  197.7 6.5 %collective-permute-start = (f32[1,8,512]{2,1,0:T(8,128)S(1)}, f32[1,8,512]{2,1,0:T(8,128)S(1)}, u32[]{:S(2)}, u32[]{:S(2)}) collective-permute-start(f32[1,8,512]{2,1,0:T(8,128)S(1)} %get-tuple-element.30), channel_id=1, source_target_pairs={{0,8},{8,16},{16,24},{24,32},{32,40},{40,48},{48,56},{56,64},{64,7... | collective-permute-start | bytes 49160 | tf_op jit(solution)/shard_map/ppermute | solution.py:19
  202.3 6.6 %collective-permute-start.1 = (f32[1,8,512]{2,1,0:T(8,128)S(1)}, f32[1,8,512]{2,1,0:T(8,128)S(1)}, u32[]{:S(2)}, u32[]{:S(2)}) collective-permute-start(f32[1,8,512]{2,1,0:T(8,128)S(1)} %get-tuple-element.31), channel_id=1, source_target_pairs={{8,0},{16,8},{24,16},{32,24},{40,32},{48,40},{56,48},{64,56},{72,6... | collective-permute-start | bytes 49160 | tf_op jit(solution)/shard_map/ppermute | solution.py:21
  208.9 2.6 collective-permute-start.2
  210.2 4.4 %collective-permute-start.3 = (f32[4,1,512]{2,1,0:T(1,128)S(1)}, f32[4,1,512]{2,1,0:T(1,128)S(1)}, u32[]{:S(2)}, u32[]{:S(2)}) collective-permute-start(f32[4,1,512]{2,1,0:T(1,128)S(1)} %get-tuple-element.27), channel_id=1, source_target_pairs={{1,0},{2,1},{3,2},{4,3},{5,4},{6,5},{7,6},{9,8},{10,9},{11,10},{12... | collective-permute-start | bytes 24584 | tf_op jit(solution)/shard_map/ppermute | solution.py:21
  285.2 6.8 %collective-permute-start.4 = (f32[1,8,512]{2,1,0:T(8,128)S(1)}, f32[1,8,512]{2,1,0:T(8,128)S(1)}, u32[]{:S(2)}, u32[]{:S(2)}) collective-permute-start(f32[1,8,512]{2,1,0:T(8,128)S(1)} %get-tuple-element.28), channel_id=1, source_target_pairs={{0,8},{8,16},{16,24},{24,32},{32,40},{40,48},{48,56},{56,64},{64,7... | collective-permute-start | bytes 49160 | tf_op jit(solution)/shard_map/ppermute | solution.py:19
  290.1 6.6 %collective-permute-start.5 = (f32[1,8,512]{2,1,0:T(8,128)S(1)}, f32[1,8,512]{2,1,0:T(8,128)S(1)}, u32[]{:S(2)}, u32[]{:S(2)}) collective-permute-start(f32[1,8,512]{2,1,0:T(8,128)S(1)} %get-tuple-element.29), channel_id=1, source_target_pairs={{8,0},{16,8},{24,16},{32,24},{40,32},{48,40},{56,48},{64,56},{72,6... | collective-permute-start | bytes 49160 | tf_op jit(solution)/shard_map/ppermute | solution.py:21
  296.7 3.2 collective-permute-start.6
  298.0 4.4 %collective-permute-start.7 = (f32[4,1,512]{2,1,0:T(1,128)S(1)}, f32[4,1,512]{2,1,0:T(1,128)S(1)}, u32[]{:S(2)}, u32[]{:S(2)}) collective-permute-start(f32[4,1,512]{2,1,0:T(1,128)S(1)} %get-tuple-element.25), channel_id=1, source_target_pairs={{1,0},{2,1},{3,2},{4,3},{5,4},{6,5},{7,6},{9,8},{10,9},{11,10},{12... | collective-permute-start | bytes 24584 | tf_op jit(solution)/shard_map/ppermute | solution.py:21
Sparse Core Ops, SparseCore 0:
  33.2 154.3 all-reduce.5
where the time goes:
time: 380 us; the launch traced here: 379 us
  waiting for transfers between devices  169 us (44%)
  blocking collectives  135 us (36%)
  other arithmetic  20.6 us (5%)
  starting transfers between devices  18.6 us (5%)
  between operations  16.3 us (4%)
  matrix products  11.7 us (3%)
  local copies, waits for them, and re-layouts  7.54 us (2%)
    psum x1, waiting for transfers between devices, body(): projected, ray_weight = lax.psum((projected, ray_weight), ('slab', 'xy'))  154 us
    psum x1, blocking collectives, body(): lax.psum(jnp.sum(step_gap * step_gap), ('slab', 'xy'))  68 us
    psum x1, blocking collectives, slope_scale(): return jnp.sqrt(lax.psum(jnp.sum(slope * slope), ('slab', 'xy')) + 1e-06)  67.1 us
    ppermute x4, waiting for transfers between devices, extended(): lax.ppermute(head, axis, [((i + 1) % count, i) for i in range(ends)])  14.8 us
    ppermute x4, starting transfers between devices, extended(): lax.ppermute(tail, axis, [(i, (i + 1) % count) for i in range(ends)])  12.1 us
  transfers between devices with their start and end apart: 9, of which 5 were waited for; matrix products, arithmetic and copies ran while one was open for 0% of the time, Pallas kernels for 0%

commit v1 on v0

v1 whole, which is shorter than its diff:
```python
import functools

import jax
import jax.numpy as jnp
from jax import lax
from jax.experimental import pallas as pl
from jax.experimental.pallas import tpu as pltpu
from jax.sharding import PartitionSpec as P

TV_RATE = 0.8
SMOOTHING = 0.01
MESH = pl.DeviceIdType.MESH
F32 = jnp.float32
BF16 = jnp.bfloat16
GROUPS = 12


def iota(shape, dim):
    return lax.broadcasted_iota(jnp.int32, shape, dim)


def lane_next(x):
    return jnp.where(iota(x.shape, 2) < x.shape[2] - 1, pltpu.roll(x, x.shape[2] - 1, 2), 0.0)


def units(field):
    base = field[:-1]
    diff_a = field[1:] - base
    diff_b = pltpu.roll(base, base.shape[1] - 1, 1) - base
    diff_e = lane_next(base) - base
    inv = lax.rsqrt(diff_a * diff_a + diff_b * diff_b + diff_e * diff_e + SMOOTHING)
    return diff_a * inv, diff_b * inv, diff_e * inv


def tv_slope(field):
    unit_a, unit_b, unit_e = units(field)
    core = field[1:-1]
    prev_b = pltpu.roll(unit_b[1:], 1, 1)
    edge = core * lax.rsqrt(core * core + SMOOTHING)
    prev_e = jnp.where(iota(core.shape, 2) == 0, edge, pltpu.roll(unit_e[1:], 1, 2))
    return unit_a[:-1] + prev_b + prev_e - (unit_a + unit_b + unit_e)[1:]


def lane_partial(x):
    rows = jnp.sum(x, axis=0)
    parts = rows[:, :128]
    for c in range(1, x.shape[2] // 128):
        parts = parts + rows[:, c * 128 : (c + 1) * 128]
    return jnp.sum(parts, axis=0, keepdims=True)


def kernel(
    ns, nx,
    vol_hbm, foot_hbm, blk_hbm, cells_hbm, meas_hbm,
    upd_ref, cor_ref,
    vol, wbuf, blk, cells, meas, bcol, ccol, onehot, contrib,
    send_a, recv_a, total, send_b, recv_b, lhs_b, num, den,
    ublk, rows_lo, rows_hi, uside, hnext, hprev,
    red_s, red_xy, red_slab,
    sem_w, sem_in, sem_s, sem_a, sem_b, sem_c, sem_cs, sem_r,
):
    s = lax.axis_index("slab")
    r = lax.axis_index("xy")
    groups = wbuf.shape[0]

    ins = [
        pltpu.make_async_copy(blk_hbm, blk, sem_in.at[0]),
        pltpu.make_async_copy(cells_hbm, cells, sem_in.at[1]),
        pltpu.make_async_copy(vol_hbm, vol, sem_in.at[2]),
        pltpu.make_async_copy(
            meas_hbm.at[:, pl.ds(pl.multiple_of((s * nx + r) * 1024, 1024), 1024)], meas, sem_in.at[3]
        ),
    ]
    for c in ins:
        c.start()

    def load(i):
        return pltpu.make_async_copy(foot_hbm.at[i], wbuf.at[i], sem_w.at[i])

    @pl.loop(0, groups)
    def _(i):
        load(i).start()

    barrier = pltpu.get_barrier_semaphore()

    def hello(ds, dr):
        pl.semaphore_signal(barrier, inc=1, device_id=(ds, dr), device_id_type=MESH)

    @pl.loop(1, nx)
    def _(d):
        rp = lax.rem(r + d, nx)
        hello(s, rp)

        @pl.when(s > 0)
        def _():
            hello(s - 1, rp)

        @pl.when(s < ns - 1)
        def _():
            hello(s + 1, rp)

    @pl.loop(1, ns)
    def _(d):
        hello(lax.rem(s + d, ns), r)

    recv_b[GROUPS:] = jnp.zeros((16 - GROUPS,) + recv_b.shape[1:], BF16)

    @pl.when(s == 0)
    def _():
        recv_b[0:2] = jnp.zeros((2,) + recv_b.shape[1:], BF16)
        uside[0] = jnp.zeros(uside.shape[1:], F32)
        hnext[0] = jnp.zeros(hnext.shape[1:], F32)
        hprev[0] = jnp.zeros(hprev.shape[1:], F32)

    @pl.when(s == ns - 1)
    def _():
        recv_b[10:12] = jnp.zeros((2,) + recv_b.shape[1:], BF16)
        uside[1] = jnp.zeros(uside.shape[1:], F32)
        hnext[2] = jnp.zeros(hnext.shape[1:], F32)
        hprev[2] = jnp.zeros(hprev.shape[1:], F32)

    @pl.when(r == 0)
    def _():
        hprev[...] = jnp.zeros(hprev.shape, F32)

    @pl.when(r == nx - 1)
    def _():
        hnext[...] = jnp.zeros(hnext.shape, F32)

    ins[0].wait()
    ins[1].wait()
    for p in range(2):
        for t in range(4):
            bcol[p, 2 * t : 2 * t + 2, 0:8] = blk[p, t]
            ccol[p, 2 * t : 2 * t + 2, 0:8] = cells[p, t]
    lane = iota((8, 128), 1)
    view4 = (iota((8, 128), 0) & 1) * 4
    first = (4 * s - 1) * 8
    for p in range(2):
        blk_p = bcol[p]
        cells_p = ccol[p]
        for x in range(8):
            i = p * 8 + x
            near = jnp.broadcast_to(blk_p[:, x : x + 1], (8, 128)) - first
            target = (near >> 2) * 8 + view4 + (near & 3)
            onehot[i * 8 : i * 8 + 8, :] = jnp.where(lane == target, 1.0, 0.0)
            den[i * 8 : i * 8 + 8, :] = jnp.broadcast_to(cells_p[:, x : x + 1], (8, 128))
    ins[2].wait()

    row16 = iota((16, 128), 0)

    @pl.loop(0, groups)
    def _(i):
        vox = vol[pl.ds(i, 1), :]
        parts = []
        for k in range(8):
            t = k // 2
            spread = jnp.broadcast_to(vox[:, t * 128 : (t + 1) * 128], (16, 128))
            parts.append(
                jnp.where(row16 == k, spread, jnp.where(row16 == k + 8, 1.0, 0.0)).astype(BF16)
            )
        left = jnp.concatenate(parts, axis=1)
        load(i).wait()
        out = jnp.dot(left, wbuf[i], preferred_element_type=F32)
        at = pl.ds(pl.multiple_of(i * 8, 8), 8)
        limit = den[at, :]
        limit = jnp.concatenate([limit, limit], axis=1)
        live = iota((8, 256), 1) < limit
        contrib[at, 0:256] = jnp.where(live, out[0:8], 0.0)
        contrib[at, 256:512] = jnp.where(live, out[8:16], 0.0)

    hot = onehot[...].astype(BF16)
    hot_t = jnp.transpose(onehot[...]).astype(BF16)
    whole = contrib[...]
    high = whole.astype(BF16)
    low = (whole - high.astype(F32)).astype(BF16)
    sums = jnp.dot(hot_t, high, preferred_element_type=F32) + jnp.dot(
        hot_t, low, preferred_element_type=F32
    )
    send_a[...] = sums.reshape(16, 8, 512)

    count = 7 + (ns - 1) + jnp.where(s > 0, nx - 1, 0) + jnp.where(s < ns - 1, nx - 1, 0)
    pl.semaphore_wait(barrier, count)

    def remote(src, dst, sem_send, sem_recv, ds, dr):
        return pltpu.make_async_remote_copy(
            src_ref=src, dst_ref=dst, send_sem=sem_send, recv_sem=sem_recv,
            device_id=(ds, dr), device_id_type=MESH,
        )

    @pl.when(s > 0)
    def _():
        for g in range(2):
            remote(send_a.at[g], recv_a.at[nx - 1 + r], sem_s.at[1], sem_a.at[1], s - 1, nx - 2 + g).start()

    @pl.when(s < ns - 1)
    def _():
        for g in range(2):
            remote(send_a.at[10 + g], recv_a.at[nx - 1 + r], sem_s.at[2], sem_a.at[1], s + 1, g).start()

    @pl.loop(1, nx)
    def _(d):
        rp = lax.rem(r + d, nx)
        remote(send_a.at[2 + rp], recv_a.at[d - 1], sem_s.at[0], sem_a.at[0], s, rp).start()

    ins[3].wait()
    m = meas[...]
    seen = jnp.concatenate(
        [m[v : v + 1, q * 256 : (q + 1) * 256] for v in range(2) for q in range(4)], axis=0
    )
    own = send_a[2 + r]
    remote(send_a.at[pl.ds(0, nx - 1)], recv_a.at[pl.ds(0, nx - 1)], sem_s.at[0], sem_a.at[0], s, r).wait_recv()
    total[...] = own + jnp.sum(recv_a[0 : nx - 1], axis=0)
    low_edge = jnp.logical_and(r < 2, s > 0)
    high_edge = jnp.logical_and(r >= nx - 2, s < ns - 1)

    @pl.when(jnp.logical_or(low_edge, high_edge))
    def _():
        remote(send_a.at[pl.ds(0, nx)], recv_a.at[pl.ds(nx - 1, nx)], sem_s.at[0], sem_a.at[1], s, r).wait_recv()
        total[...] += jnp.sum(recv_a[nx - 1 : 2 * nx - 1], axis=0)

    tot = total[...]
    corr = (seen - tot[:, 0:256]) / jnp.maximum(tot[:, 256:512], 1.0)
    send_b[...] = corr.astype(BF16)
    recv_b[2 + r] = corr.astype(BF16)

    @pl.when(low_edge)
    def _():
        @pl.loop(0, nx)
        def _(rp):
            remote(send_b, recv_b.at[10 + r], sem_s.at[4], sem_b.at[2], s - 1, rp).start()

    @pl.when(high_edge)
    def _():
        @pl.loop(0, nx)
        def _(rp):
            remote(send_b, recv_b.at[r - (nx - 2)], sem_s.at[4], sem_b.at[1], s + 1, rp).start()

    @pl.loop(1, nx)
    def _(d):
        rp = lax.rem(r + d, nx)
        remote(send_b, recv_b.at[2 + r], sem_s.at[3], sem_b.at[0], s, rp).start()

    for v in range(2):
        for q in range(4):
            cor_ref[v : v + 1, q * 256 : (q + 1) * 256] = corr[v * 4 + q : v * 4 + q + 1, :]

    limit = den[...]
    limit = jnp.concatenate([limit, limit], axis=1)
    live = iota((128, 256), 1) < limit
    live3 = jnp.where(live, 1.0, 0.0).reshape(16, 8, 256)

    remote(recv_b.at[pl.ds(0, nx - 1)], recv_b.at[pl.ds(0, nx - 1)], sem_s.at[3], sem_b.at[0], s, r).wait_recv()

    @pl.when(s > 0)
    def _():
        remote(recv_b.at[pl.ds(0, 2)], recv_b.at[pl.ds(0, 2)], sem_s.at[3], sem_b.at[1], s, r).wait_recv()

    @pl.when(s < ns - 1)
    def _():
        remote(recv_b.at[pl.ds(10, 2)], recv_b.at[pl.ds(10, 2)], sem_s.at[3], sem_b.at[2], s, r).wait_recv()

    table = recv_b[...].astype(F32).reshape(128, 256).astype(BF16)
    picked = jnp.dot(hot, table, preferred_element_type=F32)
    picked = jnp.where(live, picked, 0.0).reshape(16, 8, 256)
    lhs_b[...] = jnp.concatenate([picked, live3], axis=1).astype(BF16)

    row8 = iota((8, 128), 0)

    @pl.loop(0, 2)
    def _(p):
        tops, bottoms = [], []
        for x in range(8):
            i = p * 8 + x
            out = lax.dot_general(
                lhs_b[i], wbuf[i], (((1,), (1,)), ((), ())), preferred_element_type=F32
            )
            for rows, into in ((out[0:8], tops), (out[8:16], bottoms)):
                lanes = []
                for t in range(4):
                    k = 2 * t
                    both = jnp.where(row8 == k, rows[:, k * 128 : k * 128 + 128], 0.0) + jnp.where(
                        row8 == k + 1, rows[:, k * 128 + 128 : k * 128 + 256], 0.0
                    )
                    lanes.append(jnp.sum(both, axis=0, keepdims=True))
                into.append(jnp.concatenate(lanes, axis=1))
        num[pl.ds(pl.multiple_of(p * 8, 8), 8), :] = jnp.concatenate(tops, axis=0)
        num[pl.ds(pl.multiple_of(p * 8 + 16, 8), 8), :] = jnp.concatenate(bottoms, axis=0)

    before = vol[...]
    sart = jnp.maximum(before + num[0:groups] / num[groups : 2 * groups], 0.0)
    gap = (sart - before).reshape(2, 8, 512)
    cells3 = sart.reshape(2, 8, 512)

    ublk[...] = cells3
    rows_lo[...] = cells3[:, 0:2, :]
    rows_hi[...] = cells3[:, 6:8, :]

    def exists(ds, dr):
        ok = None
        for cond in (
            [s > 0] if ds < 0 else [s < ns - 1] if ds > 0 else []
        ) + ([r > 0] if dr < 0 else [r < nx - 1] if dr > 0 else []):
            ok = cond if ok is None else jnp.logical_and(ok, cond)
        return ok

    def halo(n, ds, dr):
        if dr == 0:
            src, dst = ublk, uside.at[1 if ds < 0 else 0]
        elif dr < 0:
            src, dst = rows_lo, hnext.at[1 - ds]
        else:
            src, dst = rows_hi, hprev.at[1 - ds]
        return remote(src, dst, sem_cs.at[n], sem_c.at[n], s + ds, r + dr)

    offsets = [(ds, dr) for ds in (-1, 1) for dr in (-1, 1, 0)] + [(0, -1), (0, 1)]
    for n, (ds, dr) in enumerate(offsets):

        @pl.when(exists(ds, dr))
        def _():
            halo(n, ds, dr).start()

    for n, (ds, dr) in enumerate(offsets):

        @pl.when(exists(-ds, -dr))
        def _():
            halo(n, ds, dr).wait_recv()

    def padded(main, after, before):
        return jnp.concatenate([main, after, jnp.zeros((4, 512), F32), before], axis=0)[None]

    field = jnp.concatenate(
        [padded(uside[0, p], hnext[0, p], hprev[0, p]) for p in range(2)]
        + [padded(ublk[p], hnext[1, p], hprev[1, p]) for p in range(2)]
        + [padded(uside[1, p], hnext[2, p], hprev[2, p]) for p in range(2)],
        axis=0,
    )
    slope = tv_slope(field)

    def reduce_all(n, parts):
        red_s[2 * n] = parts

        @pl.loop(1, nx)
        def _(d):
            rp = lax.rem(r + d, nx)
            remote(red_s.at[2 * n], red_xy.at[n, d - 1], sem_s.at[5 + 2 * n], sem_r.at[2 * n], s, rp).start()

        remote(
            red_xy.at[n, pl.ds(0, nx - 1)], red_xy.at[n, pl.ds(0, nx - 1)],
            sem_s.at[5 + 2 * n], sem_r.at[2 * n], s, r,
        ).wait_recv()
        parts = parts + jnp.sum(red_xy[n, 0 : nx - 1], axis=0)
        red_s[2 * n + 1] = parts

        @pl.loop(1, ns)
        def _(d):
            sp = lax.rem(s + d, ns)
            remote(
                red_s.at[2 * n + 1], red_slab.at[n, d - 1], sem_s.at[6 + 2 * n], sem_r.at[2 * n + 1], sp, r
            ).start()

        remote(
            red_slab.at[n, pl.ds(0, ns - 1)], red_slab.at[n, pl.ds(0, ns - 1)],
            sem_s.at[6 + 2 * n], sem_r.at[2 * n + 1], s, r,
        ).wait_recv()
        return parts + jnp.sum(red_slab[n, 0 : ns - 1], axis=0)

    own_slope = slope[1:3, 0:8, :]
    both = reduce_all(0, jnp.concatenate([lane_partial(gap * gap), lane_partial(own_slope * own_slope)], axis=1))
    rate = TV_RATE * jnp.sqrt(jnp.sum(both[:, 0:128], axis=1, keepdims=True))
    scale = jnp.sqrt(jnp.sum(both[:, 128:256], axis=1, keepdims=True) + 1e-06)
    inner = field[1:5]
    plane = iota(inner.shape, 0) + jnp.where(s > 0, 1, 0)
    row = iota(inner.shape, 1)
    inside = jnp.logical_and(plane >= 1, iota(inner.shape, 0) < jnp.where(s < ns - 1, 4, 3))
    inside = jnp.logical_and(inside, row < jnp.where(r > 0, 16, 12))
    inside = jnp.logical_and(inside, jnp.logical_or(row < 8, jnp.logical_or(row >= 12, r < nx - 1)))
    step = (rate / scale).reshape(1, 1, 1)
    first_u = jnp.where(inside, inner - step * slope, 0.0)
    slope2 = tv_slope(first_u)[:, 0:8, :]
    part2 = lane_partial(slope2 * slope2)
    both2 = reduce_all(1, jnp.concatenate([part2, part2], axis=1))
    scale2 = jnp.sqrt(jnp.sum(both2[:, 0:128], axis=1, keepdims=True) + 1e-06)
    step2 = (rate / scale2).reshape(1, 1, 1)
    upd_ref[...] = first_u[1:3, 0:8, :] - step2 * slope2

    remote(send_a.at[pl.ds(0, nx - 1)], recv_a.at[pl.ds(0, nx - 1)], sem_s.at[0], sem_a.at[0], s, r).wait_send()
    remote(recv_b.at[pl.ds(0, nx - 1)], recv_b.at[pl.ds(0, nx - 1)], sem_s.at[3], sem_b.at[0], s, r).wait_send()

    @pl.when(s > 0)
    def _():
        remote(send_a.at[pl.ds(0, 2)], recv_a.at[pl.ds(0, 2)], sem_s.at[1], sem_a.at[0], s, r).wait_send()

    @pl.when(s < ns - 1)
    def _():
        remote(send_a.at[pl.ds(0, 2)], recv_a.at[pl.ds(0, 2)], sem_s.at[2], sem_a.at[0], s, r).wait_send()

    @pl.when(jnp.logical_or(low_edge, high_edge))
    def _():
        remote(recv_b.at[pl.ds(0, nx)], recv_b.at[pl.ds(0, nx)], sem_s.at[4], sem_b.at[0], s, r).wait_send()

    for n, (ds, dr) in enumerate(offsets):

        @pl.when(exists(ds, dr))
        def _():
            halo(n, ds, dr).wait_send()

    for n in range(2):
        remote(
            red_xy.at[n, pl.ds(0, nx - 1)], red_xy.at[n, pl.ds(0, nx - 1)],
            sem_s.at[5 + 2 * n], sem_r.at[0], s, r,
        ).wait_send()
        remote(
            red_slab.at[n, pl.ds(0, ns - 1)], red_slab.at[n, pl.ds(0, ns - 1)],
            sem_s.at[6 + 2 * n], sem_r.at[0], s, r,
        ).wait_send()


def body(ns, nx, volume, footprint, tile_block, tile_cells, measured):
    any_space = pl.BlockSpec(memory_space=pltpu.HBM)
    vmem = pl.BlockSpec(memory_space=pltpu.VMEM)
    dma = pltpu.SemaphoreType.DMA
    call = pl.pallas_call(
        functools.partial(kernel, ns, nx),
        out_shape=(
            jax.ShapeDtypeStruct((2, 8, 512), F32),
            jax.ShapeDtypeStruct((2, 1024), F32),
        ),
        in_specs=[any_space] * 5,
        out_specs=(vmem, vmem),
        scratch_shapes=[
            pltpu.VMEM((16, 512), F32),
            pltpu.VMEM((16, 1024, 256), BF16),
            pltpu.VMEM((2, 4, 2, 8), jnp.int32),
            pltpu.VMEM((2, 4, 2, 8), jnp.int32),
            pltpu.VMEM((2, 1024), F32),
            pltpu.VMEM((2, 8, 128), jnp.int32),
            pltpu.VMEM((2, 8, 128), jnp.int32),
            pltpu.VMEM((128, 128), F32),
            pltpu.VMEM((128, 512), F32),
            pltpu.VMEM((16, 8, 512), F32),
            pltpu.VMEM((2 * nx - 1, 8, 512), F32),
            pltpu.VMEM((8, 512), F32),
            pltpu.VMEM((8, 256), BF16),
            pltpu.VMEM((16, 8, 256), BF16),
            pltpu.VMEM((16, 16, 256), BF16),
            pltpu.VMEM((32, 512), F32),
            pltpu.VMEM((128, 128), jnp.int32),
            pltpu.VMEM((2, 8, 512), F32),
            pltpu.VMEM((2, 2, 512), F32),
            pltpu.VMEM((2, 2, 512), F32),
            pltpu.VMEM((2, 2, 8, 512), F32),
            pltpu.VMEM((3, 2, 2, 512), F32),
            pltpu.VMEM((3, 2, 2, 512), F32),
            pltpu.VMEM((4, 1, 256), F32),
            pltpu.VMEM((2, nx - 1, 1, 256), F32),
            pltpu.VMEM((2, ns - 1, 1, 256), F32),
            dma((16,)),
            dma((4,)),
            dma((9,)),
            dma((2,)),
            dma((3,)),
            dma((8,)),
            dma((8,)),
            dma((4,)),
        ],
        compiler_params=pltpu.CompilerParams(
            collective_id=0, has_side_effects=True, vmem_limit_bytes=24 * 1024 * 1024
        ),
    )
    return call(
        volume.reshape(16, 512),
        footprint.reshape(16, 1024, 256),
        jnp.transpose(tile_block, (0, 2, 3, 1)),
        jnp.transpose(tile_cells, (0, 2, 3, 1)),
        measured,
    )


def solution(mesh):
    ns, nx = mesh.shape["slab"], mesh.shape["xy"]
    placed = (
        P("slab", "xy", None),
        P("slab", "xy", None, None, None, None),
        P("slab", "xy", None, None),
        P("slab", "xy", None, None),
        P(),
    )
    return jax.shard_map(
        functools.partial(body, ns, nx),
        mesh=mesh,
        in_specs=placed,
        out_specs=(P("slab", "xy", None), P(None, ("slab", "xy"))),
        check_vma=False,
    )
```

time: 380 us -> 53.3 us (0.14)
  waiting for transfers between devices: 169 us -> 0 us
  blocking collectives: 135 us -> 0 us
  Pallas kernels: 0 us -> 44.3 us
  other arithmetic: 20.6 us -> 0 us
  starting transfers between devices: 18.6 us -> 0 us
  between operations: 16.3 us -> 0.65 us
  matrix products: 11.7 us -> 0 us
    psum x1 -> x0, waiting for transfers between devices: 154 us -> none  [body(): projected, ray_weight = lax.psum((projected, ray_weight), ('slab', 'xy'))]
    psum x2 -> x0, blocking collectives: 135 us -> none  [the longest x1 68 us: body(): lax.psum(jnp.sum(step_gap * step_gap), ('slab', 'xy'))]
    pallas_call x0 -> x1, Pallas kernels: none -> 44.3 us  [body(): call(volume.reshape(16, 512), footprint.reshape(16, 1024, 256), jnp.trans...]
    ppermute x8 -> x0, starting transfers between devices: 18.5 us -> none  [the longest x4 12.1 us: extended(): lax.ppermute(tail, axis, [(i, (i + 1) % count) for i in range(ends)])]
    ppermute x8 -> x0, waiting for transfers between devices: 14.8 us -> none  [the longest x4 14.8 us: extended(): lax.ppermute(head, axis, [((i + 1) % count, i) for i in range(ends)])]
    dot_general x4 -> x0, matrix products: 11.7 us -> none  [the longest x1 5.63 us: body(): jnp.einsum('tvjc,tvc->tj', masked, picked, preferred_element_type=jnp.flo...]
    reduce_sum x4 -> x0, other arithmetic: 8.07 us -> none  [the longest x1 6.02 us: body(): column = jnp.sum(masked, axis=(1, 3), dtype=jnp.float32)]
    select_n x1 -> x0, other arithmetic: 7.31 us -> none  [body(): jnp.where(live[:, :, None, :], weights, jnp.zeros((), jnp.bfloat16))]
  transfers between devices with their start and end apart: 9 -> 0, of which waited for: 5 -> 0; matrix products, arithmetic and copies ran while one was open for 0% -> 0% of each run, Pallas kernels for 0% -> 0%
where the time goes in v1:
time: 53.3 us; the launch traced here: 52.9 us
  Pallas kernels  44.3 us (83%)
  local copies, waits for them, and re-layouts  7.96 us (15%)
  between operations  0.65 us (1%)
    pallas_call x1, Pallas kernels, body(): call(volume.reshape(16, 512), footprint.reshape(16, 1024, 256), jnp.trans...  44.3 us
    unnamed x12, local copies, waits for them, and re-layouts  7.96 us

profile of v1, /device:TPU:1, one launch (start us, length us, event | category | flops | bytes accessed | tf_op | source)
XLA Modules:
  0.0 52.9 jit_solution(3216882990888812644)
XLA Ops:
  0.6 0.0 copy-start
  0.6 3.4 %copy-done = bf16[2,8,4,2,128,256]{5,4,3,2,1,0:T(8,128)(2,1)S(1)} copy-done((bf16[2,8,4,2,128,256]{5,4,3,2,1,0:T(8,128)(2,1)S(1)}, bf16[2,8,4,2,128,256]{5,4,3,2,1,0:T(8,128)(2,1)}, u32[]{:S(2)}) %copy-start) | copy-done | bytes 8388632
  4.0 0.0 copy-start.1
  4.0 1.2 %copy-done.1 = f32[2,131072]{1,0:T(2,128)S(1)} copy-done((f32[2,131072]{1,0:T(2,128)S(1)}, f32[2,131072]{1,0:T(2,128)}, u32[]{:S(2)}) %copy-start.1) | copy-done | bytes 1048600
  5.2 0.0 copy-start.2
  5.2 0.8 %copy-done.2 = f32[2,8,512]{2,1,0:T(8,128)S(1)} copy-done((f32[2,8,512]{2,1,0:T(8,128)S(1)}, f32[2,8,512]{2,1,0:T(8,128)}, u32[]{:S(2)}) %copy-start.2) | copy-done | bytes 32792
  6.0 0.0 copy-start.3
  6.0 0.7 %copy-done.3 = s32[2,8,4,2]{1,3,2,0:T(2,128)S(1)} copy-done((s32[2,8,4,2]{1,3,2,0:T(2,128)S(1)}, s32[2,8,4,2]{1,3,2,0:T(2,128)}, u32[]{:S(2)}) %copy-start.3) | copy-done | bytes 536
  6.7 0.0 copy-start.4
  6.7 0.7 %copy-done.4 = s32[2,8,4,2]{1,3,2,0:T(2,128)S(1)} copy-done((s32[2,8,4,2]{1,3,2,0:T(2,128)S(1)}, s32[2,8,4,2]{1,3,2,0:T(2,128)}, u32[]{:S(2)}) %copy-start.4) | copy-done | bytes 536
  7.4 44.3 %shard_map.68 = (f32[2,8,512]{2,1,0:T(8,128)S(1)}, f32[2,1024]{1,0:T(2,128)S(1)}) custom-call(f32[16,512]{1,0:T(8,128)S(1)} %bitcast.5, bf16[16,1024,256]{2,1,0:T(8,128)(2,1)S(1)} %bitcast.4, s32[2,4,2,8]{3,2,1,0:T(2,128)S(1)} %bitcast.6, s32[2,4,2,8]{3,2,1,0:T(2,128)S(1)} %bitcast.7, f32[2,131072]{1,0:T(2,128)S(1)} %copy-done.1), custom_call_target="tpu_custom_call" | custom-call | tf_op jit(solution)/shard_map/pallas_call | solution.py:471
  51.7 0.6 %copy.9 = f32[2,8,512]{2,1,0:T(8,128)} copy(f32[2,8,512]{2,1,0:T(8,128)S(1)} %get-tuple-element.4) | data formatting | bytes 65536
  52.3 0.6 %copy.10 = f32[2,1024]{1,0:T(2,128)} copy(f32[2,1024]{1,0:T(2,128)S(1)} %get-tuple-element.5) | data formatting | bytes 16384
Async XLA Ops:
  0.6 3.4 %copy-start = (bf16[2,8,4,2,128,256]{5,4,3,2,1,0:T(8,128)(2,1)S(1)}, bf16[2,8,4,2,128,256]{5,4,3,2,1,0:T(8,128)(2,1)}, u32[]{:S(2)}) copy-start(bf16[2,8,4,2,128,256]{5,4,3,2,1,0:T(8,128)(2,1)} %param.6) | copy-start | bytes 25165828
  4.0 1.2 %copy-start.1 = (f32[2,131072]{1,0:T(2,128)S(1)}, f32[2,131072]{1,0:T(2,128)}, u32[]{:S(2)}) copy-start(f32[2,131072]{1,0:T(2,128)} %meas_hbm.1) | copy-start | bytes 3145732
  5.2 0.8 %copy-start.2 = (f32[2,8,512]{2,1,0:T(8,128)S(1)}, f32[2,8,512]{2,1,0:T(8,128)}, u32[]{:S(2)}) copy-start(f32[2,8,512]{2,1,0:T(8,128)} %param.5) | copy-start | bytes 98308
  6.0 0.7 %copy-start.3 = (s32[2,8,4,2]{1,3,2,0:T(2,128)S(1)}, s32[2,8,4,2]{1,3,2,0:T(2,128)}, u32[]{:S(2)}) copy-start(s32[2,8,4,2]{1,3,2,0:T(2,128)} %param.7) | copy-start | bytes 1540
  6.7 0.7 %copy-start.4 = (s32[2,8,4,2]{1,3,2,0:T(2,128)S(1)}, s32[2,8,4,2]{1,3,2,0:T(2,128)}, u32[]{:S(2)}) copy-start(s32[2,8,4,2]{1,3,2,0:T(2,128)} %param.8) | copy-start | bytes 1540

commit v2 on v1

--- a/solution.py
+++ b/solution.py
@@ -49,6 +49,25 @@
     return jnp.sum(parts, axis=0, keepdims=True)
 
 
+def everyone_else(ns, nx, s, r):
+    if (ns, nx) != (16, 8):
+        return [(lax.rem(s + d // nx, ns), lax.rem(r + d % nx, nx)) for d in range(1, ns * nx)]
+    z = ((s // 2) % 2) * 2 + r // 4
+    at_x = [((s // 4 + d) % 4) * 4 for d in range(4)]
+    at_z = [(z + d) % 4 for d in range(4)]
+    at_y = [(r + d) % 4 for d in range(4)]
+    at_core = [(s + d) % 2 for d in range(2)]
+    slab_z = [(v // 2) * 2 for v in at_z]
+    xy_z = [(v % 2) * 4 for v in at_z]
+    slab = {
+        (dx, dz, dc): at_x[dx] + slab_z[dz] + at_core[dc] for dx in range(4) for dz in range(4) for dc in range(2)
+    }
+    xy = {(dz, dy): xy_z[dz] + at_y[dy] for dz in range(4) for dy in range(4)}
+    moves = [(dx, dz, dy, dc) for dx in range(4) for dz in range(4) for dy in range(4) for dc in range(2)]
+    moves.sort(key=lambda m: -sum(min(d, 4 - d) for d in m[:3]) * 2 - m[3])
+    return [(slab[dx, dz, dc], xy[dz, dy]) for dx, dz, dy, dc in moves if (dx, dz, dy, dc) != (0, 0, 0, 0)]
+
+
 def kernel(
     ns, nx,
     vol_hbm, foot_hbm, blk_hbm, cells_hbm, meas_hbm,
@@ -56,12 +75,15 @@
     vol, wbuf, blk, cells, meas, bcol, ccol, onehot, contrib,
     send_a, recv_a, total, send_b, recv_b, lhs_b, num, den,
     ublk, rows_lo, rows_hi, uside, hnext, hprev,
-    red_s, red_xy, red_slab,
+    red_s, red_in,
     sem_w, sem_in, sem_s, sem_a, sem_b, sem_c, sem_cs, sem_r,
 ):
     s = lax.axis_index("slab")
     r = lax.axis_index("xy")
     groups = wbuf.shape[0]
+    low_edge = jnp.logical_and(r < 2, s > 0)
+    high_edge = jnp.logical_and(r >= nx - 2, s < ns - 1)
+    pending = []
 
     ins = [
         pltpu.make_async_copy(blk_hbm, blk, sem_in.at[0]),
@@ -83,25 +105,9 @@
 
     barrier = pltpu.get_barrier_semaphore()
 
-    def hello(ds, dr):
+    others = everyone_else(ns, nx, s, r)
+    for ds, dr in others:
         pl.semaphore_signal(barrier, inc=1, device_id=(ds, dr), device_id_type=MESH)
-
-    @pl.loop(1, nx)
-    def _(d):
-        rp = lax.rem(r + d, nx)
-        hello(s, rp)
-
-        @pl.when(s > 0)
-        def _():
-            hello(s - 1, rp)
-
-        @pl.when(s < ns - 1)
-        def _():
-            hello(s + 1, rp)
-
-    @pl.loop(1, ns)
-    def _(d):
-        hello(lax.rem(s + d, ns), r)
 
     recv_b[GROUPS:] = jnp.zeros((16 - GROUPS,) + recv_b.shape[1:], BF16)
 
@@ -179,8 +185,7 @@
     )
     send_a[...] = sums.reshape(16, 8, 512)
 
-    count = 7 + (ns - 1) + jnp.where(s > 0, nx - 1, 0) + jnp.where(s < ns - 1, nx - 1, 0)
-    pl.semaphore_wait(barrier, count)
+    pl.semaphore_wait(barrier, len(others))
 
     def remote(src, dst, sem_send, sem_recv, ds, dr):
         return pltpu.make_async_remote_copy(
@@ -203,6 +208,15 @@
         rp = lax.rem(r + d, nx)
         remote(send_a.at[2 + rp], recv_a.at[d - 1], sem_s.at[0], sem_a.at[0], s, rp).start()
 
+    def sent(ref, sem, cond=None):
+        def wait():
+            remote(ref, ref, sem, sem_a.at[0], s, r).wait_send()
+
+        pending.append(wait if cond is None else lambda: pl.when(cond)(wait))
+
+    sent(recv_a.at[pl.ds(0, nx - 1)], sem_s.at[0])
+    sent(recv_a.at[pl.ds(0, 2)], sem_s.at[1], s > 0)
+    sent(recv_a.at[pl.ds(0, 2)], sem_s.at[2], s < ns - 1)
     ins[3].wait()
     m = meas[...]
     seen = jnp.concatenate(
@@ -211,8 +225,6 @@
     own = send_a[2 + r]
     remote(send_a.at[pl.ds(0, nx - 1)], recv_a.at[pl.ds(0, nx - 1)], sem_s.at[0], sem_a.at[0], s, r).wait_recv()
     total[...] = own + jnp.sum(recv_a[0 : nx - 1], axis=0)
-    low_edge = jnp.logical_and(r < 2, s > 0)
-    high_edge = jnp.logical_and(r >= nx - 2, s < ns - 1)
 
     @pl.when(jnp.logical_or(low_edge, high_edge))
     def _():
@@ -241,6 +253,8 @@
         rp = lax.rem(r + d, nx)
         remote(send_b, recv_b.at[2 + r], sem_s.at[3], sem_b.at[0], s, rp).start()
 
+    sent(recv_b.at[pl.ds(0, nx - 1)], sem_s.at[3])
+    sent(recv_b.at[pl.ds(0, nx)], sem_s.at[4], jnp.logical_or(low_edge, high_edge))
     for v in range(2):
         for q in range(4):
             cor_ref[v : v + 1, q * 256 : (q + 1) * 256] = corr[v * 4 + q : v * 4 + q + 1, :]
@@ -320,6 +334,10 @@
         def _():
             halo(n, ds, dr).start()
 
+        pending.append(
+            lambda n=n, ds=ds, dr=dr: pl.when(exists(ds, dr))(lambda: halo(n, ds, dr).wait_send())
+        )
+
     for n, (ds, dr) in enumerate(offsets):
 
         @pl.when(exists(-ds, -dr))
@@ -338,37 +356,23 @@
     slope = tv_slope(field)
 
     def reduce_all(n, parts):
-        red_s[2 * n] = parts
-
-        @pl.loop(1, nx)
-        def _(d):
-            rp = lax.rem(r + d, nx)
-            remote(red_s.at[2 * n], red_xy.at[n, d - 1], sem_s.at[5 + 2 * n], sem_r.at[2 * n], s, rp).start()
-
-        remote(
-            red_xy.at[n, pl.ds(0, nx - 1)], red_xy.at[n, pl.ds(0, nx - 1)],
-            sem_s.at[5 + 2 * n], sem_r.at[2 * n], s, r,
-        ).wait_recv()
-        parts = parts + jnp.sum(red_xy[n, 0 : nx - 1], axis=0)
-        red_s[2 * n + 1] = parts
-
-        @pl.loop(1, ns)
-        def _(d):
-            sp = lax.rem(s + d, ns)
-            remote(
-                red_s.at[2 * n + 1], red_slab.at[n, d - 1], sem_s.at[6 + 2 * n], sem_r.at[2 * n + 1], sp, r
-            ).start()
-
-        remote(
-            red_slab.at[n, pl.ds(0, ns - 1)], red_slab.at[n, pl.ds(0, ns - 1)],
-            sem_s.at[6 + 2 * n], sem_r.at[2 * n + 1], s, r,
-        ).wait_recv()
-        return parts + jnp.sum(red_slab[n, 0 : ns - 1], axis=0)
+        red_s[n] = parts
+        for j, (ds, dr) in enumerate(others):
+            remote(red_s.at[n], red_in.at[n, j], sem_s.at[5 + n], sem_r.at[n], ds, dr).start()
+        sent(red_in.at[n], sem_s.at[5 + n])
+        remote(red_in.at[n], red_in.at[n], sem_s.at[5 + n], sem_r.at[n], s, r).wait_recv()
+        return parts + jnp.sum(red_in[n], axis=0)
+
+    def half(x):
+        return x + pltpu.roll(x, 64, 1)
 
     own_slope = slope[1:3, 0:8, :]
-    both = reduce_all(0, jnp.concatenate([lane_partial(gap * gap), lane_partial(own_slope * own_slope)], axis=1))
-    rate = TV_RATE * jnp.sqrt(jnp.sum(both[:, 0:128], axis=1, keepdims=True))
-    scale = jnp.sqrt(jnp.sum(both[:, 128:256], axis=1, keepdims=True) + 1e-06)
+    left = iota((1, 128), 1) < 64
+    both = reduce_all(
+        0, jnp.where(left, half(lane_partial(gap * gap)), half(lane_partial(own_slope * own_slope)))
+    )
+    rate = TV_RATE * jnp.sqrt(jnp.sum(jnp.where(left, both, 0.0), axis=1, keepdims=True))
+    scale = jnp.sqrt(jnp.sum(jnp.where(left, 0.0, both), axis=1, keepdims=True) + 1e-06)
     inner = field[1:5]
     plane = iota(inner.shape, 0) + jnp.where(s > 0, 1, 0)
     row = iota(inner.shape, 1)
@@ -378,42 +382,13 @@
     step = (rate / scale).reshape(1, 1, 1)
     first_u = jnp.where(inside, inner - step * slope, 0.0)
     slope2 = tv_slope(first_u)[:, 0:8, :]
-    part2 = lane_partial(slope2 * slope2)
-    both2 = reduce_all(1, jnp.concatenate([part2, part2], axis=1))
-    scale2 = jnp.sqrt(jnp.sum(both2[:, 0:128], axis=1, keepdims=True) + 1e-06)
+    both2 = reduce_all(1, lane_partial(slope2 * slope2))
+    scale2 = jnp.sqrt(jnp.sum(both2, axis=1, keepdims=True) + 1e-06)
     step2 = (rate / scale2).reshape(1, 1, 1)
     upd_ref[...] = first_u[1:3, 0:8, :] - step2 * slope2
 
-    remote(send_a.at[pl.ds(0, nx - 1)], recv_a.at[pl.ds(0, nx - 1)], sem_s.at[0], sem_a.at[0], s, r).wait_send()
-    remote(recv_b.at[pl.ds(0, nx - 1)], recv_b.at[pl.ds(0, nx - 1)], sem_s.at[3], sem_b.at[0], s, r).wait_send()
-
-    @pl.when(s > 0)
-    def _():
-        remote(send_a.at[pl.ds(0, 2)], recv_a.at[pl.ds(0, 2)], sem_s.at[1], sem_a.at[0], s, r).wait_send()
-
-    @pl.when(s < ns - 1)
-    def _():
-        remote(send_a.at[pl.ds(0, 2)], recv_a.at[pl.ds(0, 2)], sem_s.at[2], sem_a.at[0], s, r).wait_send()
-
-    @pl.when(jnp.logical_or(low_edge, high_edge))
-    def _():
-        remote(recv_b.at[pl.ds(0, nx)], recv_b.at[pl.ds(0, nx)], sem_s.at[4], sem_b.at[0], s, r).wait_send()
-
-    for n, (ds, dr) in enumerate(offsets):
-
-        @pl.when(exists(ds, dr))
-        def _():
-            halo(n, ds, dr).wait_send()
-
-    for n in range(2):
-        remote(
-            red_xy.at[n, pl.ds(0, nx - 1)], red_xy.at[n, pl.ds(0, nx - 1)],
-            sem_s.at[5 + 2 * n], sem_r.at[0], s, r,
-        ).wait_send()
-        remote(
-            red_slab.at[n, pl.ds(0, ns - 1)], red_slab.at[n, pl.ds(0, ns - 1)],
-            sem_s.at[6 + 2 * n], sem_r.at[0], s, r,
-        ).wait_send()
+    for wait in pending:
+        wait()
 
 
 def body(ns, nx, volume, footprint, tile_block, tile_cells, measured):
@@ -452,20 +427,19 @@
             pltpu.VMEM((2, 2, 8, 512), F32),
             pltpu.VMEM((3, 2, 2, 512), F32),
             pltpu.VMEM((3, 2, 2, 512), F32),
-            pltpu.VMEM((4, 1, 256), F32),
-            pltpu.VMEM((2, nx - 1, 1, 256), F32),
-            pltpu.VMEM((2, ns - 1, 1, 256), F32),
+            pltpu.VMEM((2, 1, 128), F32),
+            pltpu.VMEM((2, ns * nx - 1, 1, 128), F32),
             dma((16,)),
             dma((4,)),
-            dma((9,)),
+            dma((7,)),
             dma((2,)),
             dma((3,)),
             dma((8,)),
             dma((8,)),
-            dma((4,)),
+            dma((2,)),
         ],
         compiler_params=pltpu.CompilerParams(
-            collective_id=0, has_side_effects=True, vmem_limit_bytes=24 * 1024 * 1024
+            collective_id=0, has_side_effects=True, vmem_limit_bytes=60 * 1024 * 1024
         ),
     )
     return call(

time: 53.3 us -> 43 us (0.81)
  local copies, waits for them, and re-layouts: 7.96 us -> 2.67 us
  Pallas kernels: 44.3 us -> 39.5 us
    unnamed x12 -> x2, local copies, waits for them, and re-layouts: 7.96 us -> 2.67 us
    pallas_call x1, Pallas kernels: 44.3 us -> 39.5 us  [body(): call(volume.reshape(16, 512), footprint.reshape(16, 1024, 256), jnp.trans...]
where the time goes in v2:
time: 43 us; the launch traced here: 42.8 us
  Pallas kernels  39.5 us (92%)
  local copies, waits for them, and re-layouts  2.67 us (6%)
  between operations  0.64 us (1%)
    pallas_call x1, Pallas kernels, body(): call(volume.reshape(16, 512), footprint.reshape(16, 1024, 256), jnp.trans...  39.5 us
    unnamed x2, local copies, waits for them, and re-layouts  2.67 us

profile of v2, /device:TPU:1, one launch (start us, length us, event | category | flops | bytes accessed | tf_op | source)
XLA Modules:
  0.0 42.8 jit_solution(4871857282278459701)
XLA Ops:
  0.6 39.5 %shard_map.68 = (f32[2,8,512]{2,1,0:T(8,128)}, f32[2,1024]{1,0:T(2,128)}) custom-call(f32[16,512]{1,0:T(8,128)} %bitcast.5, bf16[16,1024,256]{2,1,0:T(8,128)(2,1)} %bitcast.4, s32[2,4,2,8]{3,2,1,0:T(2,128)} %bitcast.6, s32[2,4,2,8]{3,2,1,0:T(2,128)} %bitcast.7, f32[2,131072]{1,0:T(2,128)} %meas_hbm.1), custom_call_target="tpu_custom_call" | custom-call | tf_op jit(solution)/shard_map/pallas_call | solution.py:445
  40.1 1.4 %copy.9 = f32[2,8,512]{2,1,0:T(8,128)} copy(f32[2,8,512]{2,1,0:T(8,128)} %get-tuple-element.4) | data formatting | bytes 65536
  41.5 1.3 %copy.10 = f32[2,1024]{1,0:T(2,128)} copy(f32[2,1024]{1,0:T(2,128)} %get-tuple-element.5) | data formatting | bytes 16384

commit v3 on v2

--- a/solution.py
+++ b/solution.py
@@ -391,16 +391,21 @@
         wait()
 
 
+def put_out(upd, cor, upd_hbm, cor_hbm, sem):
+    copies = [pltpu.make_async_copy(upd, upd_hbm, sem.at[0]), pltpu.make_async_copy(cor, cor_hbm, sem.at[1])]
+    for c in copies:
+        c.start()
+    for c in copies:
+        c.wait()
+
+
 def body(ns, nx, volume, footprint, tile_block, tile_cells, measured):
     any_space = pl.BlockSpec(memory_space=pltpu.HBM)
     vmem = pl.BlockSpec(memory_space=pltpu.VMEM)
     dma = pltpu.SemaphoreType.DMA
     call = pl.pallas_call(
         functools.partial(kernel, ns, nx),
-        out_shape=(
-            jax.ShapeDtypeStruct((2, 8, 512), F32),
-            jax.ShapeDtypeStruct((2, 1024), F32),
-        ),
+        out_shape=(pltpu.VMEM((2, 8, 512), F32), pltpu.VMEM((2, 1024), F32)),
         in_specs=[any_space] * 5,
         out_specs=(vmem, vmem),
         scratch_shapes=[
@@ -442,13 +447,22 @@
             collective_id=0, has_side_effects=True, vmem_limit_bytes=60 * 1024 * 1024
         ),
     )
-    return call(
+    operands = (
         volume.reshape(16, 512),
         footprint.reshape(16, 1024, 256),
         jnp.transpose(tile_block, (0, 2, 3, 1)),
         jnp.transpose(tile_cells, (0, 2, 3, 1)),
         measured,
     )
+    results = call(*[pltpu.with_memory_space_constraint(x, pltpu.HBM) for x in operands])
+    return pl.pallas_call(
+        put_out,
+        out_shape=tuple(jax.ShapeDtypeStruct(x.shape, F32) for x in results),
+        in_specs=[vmem, vmem],
+        out_specs=(any_space, any_space),
+        scratch_shapes=[dma((2,))],
+        compiler_params=pltpu.CompilerParams(vmem_limit_bytes=1024 * 1024),
+    )(*[pltpu.with_memory_space_constraint(x, pltpu.VMEM) for x in results])
 
 
 def solution(mesh):

time: 43 us -> 40.2 us (0.935)
  local copies, waits for them, and re-layouts: 2.67 us -> 0 us
    unnamed x2 -> x0, local copies, waits for them, and re-layouts: 2.67 us -> none
    pallas_call x1 -> x2, Pallas kernels: 39.5 us -> 39.5 us  [the longest x1 38.8 us: body(): call(*[pltpu.with_memory_space_constraint(x, pltpu.HBM) for x in operands])]
where the time goes in v3:
time: 40.2 us; the launch traced here: 40.1 us
  Pallas kernels  39.5 us (98%)
  between operations  0.64 us (2%)
    pallas_call x1, Pallas kernels, body(): call(*[pltpu.with_memory_space_constraint(x, pltpu.HBM) for x in operands])  38.8 us

profile of v3, /device:TPU:1, one launch (start us, length us, event | category | flops | bytes accessed | tf_op | source)
XLA Modules:
  0.0 40.1 jit_solution(16887813450122913290)
XLA Ops:
  0.6 38.8 %shard_map.68 = (f32[2,8,512]{2,1,0:T(8,128)S(1)}, f32[2,1024]{1,0:T(2,128)S(1)}) custom-call(f32[16,512]{1,0:T(8,128)} %bitcast.5, bf16[16,1024,256]{2,1,0:T(8,128)(2,1)} %bitcast.4, s32[2,4,2,8]{3,2,1,0:T(2,128)} %bitcast.6, s32[2,4,2,8]{3,2,1,0:T(2,128)} %bitcast.7, f32[2,131072]{1,0:T(2,128)} %meas_hbm.1), custom_call_target="tpu_custom_call" | custom-call | tf_op jit(solution)/shard_map/pallas_call | solution.py:457
  39.5 0.6 %shard_map.69 = (f32[2,8,512]{2,1,0:T(8,128)}, f32[2,1024]{1,0:T(2,128)}) custom-call(f32[2,8,512]{2,1,0:T(8,128)S(1)} %get-tuple-element.4.upd, f32[2,1024]{1,0:T(2,128)S(1)} %get-tuple-element.5.cor), custom_call_target="tpu_custom_call" | custom-call | tf_op jit(solution)/shard_map/pallas_call | solution.py:458

commit v4 on v3

--- a/solution.py
+++ b/solution.py
@@ -12,6 +12,7 @@
 MESH = pl.DeviceIdType.MESH
 F32 = jnp.float32
 BF16 = jnp.bfloat16
+PIECES = ((0, 4), (4, 8), (8, 12), (12, 16))
 GROUPS = 12
 
 
@@ -72,11 +73,11 @@
     ns, nx,
     vol_hbm, foot_hbm, blk_hbm, cells_hbm, meas_hbm,
     upd_ref, cor_ref,
-    vol, wbuf, blk, cells, meas, bcol, ccol, onehot, contrib,
+    vol, wbuf, blk, cells, meas, bcol, ccol, onehot, onehot_t, contrib,
     send_a, recv_a, total, send_b, recv_b, lhs_b, num, den,
-    ublk, rows_lo, rows_hi, uside, hnext, hprev,
+    ublk, uside, halo,
     red_s, red_in,
-    sem_w, sem_in, sem_s, sem_a, sem_b, sem_c, sem_cs, sem_r,
+    sem_w, sem_in, sem_s, sem_a, sem_b, sem_c, sem_cs, sem_r, sem_k,
 ):
     s = lax.axis_index("slab")
     r = lax.axis_index("xy")
@@ -96,42 +97,35 @@
     for c in ins:
         c.start()
 
-    def load(i):
-        return pltpu.make_async_copy(foot_hbm.at[i], wbuf.at[i], sem_w.at[i])
-
-    @pl.loop(0, groups)
-    def _(i):
-        load(i).start()
+    def load(n):
+        first, last = PIECES[n]
+        at = pl.ds(first, last - first)
+        return pltpu.make_async_copy(foot_hbm.at[at], wbuf.at[at], sem_w.at[n])
+
+    for n in range(len(PIECES)):
+        load(n).start()
 
     barrier = pltpu.get_barrier_semaphore()
 
-    others = everyone_else(ns, nx, s, r)
-    for ds, dr in others:
+    def hello(ds, dr):
         pl.semaphore_signal(barrier, inc=1, device_id=(ds, dr), device_id_type=MESH)
 
-    recv_b[GROUPS:] = jnp.zeros((16 - GROUPS,) + recv_b.shape[1:], BF16)
-
-    @pl.when(s == 0)
-    def _():
-        recv_b[0:2] = jnp.zeros((2,) + recv_b.shape[1:], BF16)
-        uside[0] = jnp.zeros(uside.shape[1:], F32)
-        hnext[0] = jnp.zeros(hnext.shape[1:], F32)
-        hprev[0] = jnp.zeros(hprev.shape[1:], F32)
-
-    @pl.when(s == ns - 1)
-    def _():
-        recv_b[10:12] = jnp.zeros((2,) + recv_b.shape[1:], BF16)
-        uside[1] = jnp.zeros(uside.shape[1:], F32)
-        hnext[2] = jnp.zeros(hnext.shape[1:], F32)
-        hprev[2] = jnp.zeros(hprev.shape[1:], F32)
-
-    @pl.when(r == 0)
-    def _():
-        hprev[...] = jnp.zeros(hprev.shape, F32)
-
-    @pl.when(r == nx - 1)
-    def _():
-        hnext[...] = jnp.zeros(hnext.shape, F32)
+    recv_b[...] = jnp.zeros(recv_b.shape, BF16)
+    uside[...] = jnp.zeros(uside.shape, F32)
+    halo[...] = jnp.zeros(halo.shape, F32)
+
+    @pl.when(s > 0)
+    def _():
+        for d in range(nx):
+            hello(s - 1, d)
+
+    @pl.when(s < ns - 1)
+    def _():
+        for d in range(nx):
+            hello(s + 1, d)
+
+    for d in range(1, nx):
+        hello(s, lax.rem(r + d, nx))
 
     ins[0].wait()
     ins[1].wait()
@@ -142,6 +136,7 @@
     lane = iota((8, 128), 1)
     view4 = (iota((8, 128), 0) & 1) * 4
     first = (4 * s - 1) * 8
+    hots = []
     for p in range(2):
         blk_p = bcol[p]
         cells_p = ccol[p]
@@ -149,43 +144,53 @@
             i = p * 8 + x
             near = jnp.broadcast_to(blk_p[:, x : x + 1], (8, 128)) - first
             target = (near >> 2) * 8 + view4 + (near & 3)
-            onehot[i * 8 : i * 8 + 8, :] = jnp.where(lane == target, 1.0, 0.0)
+            hots.append(jnp.where(lane == target, 1.0, 0.0))
             den[i * 8 : i * 8 + 8, :] = jnp.broadcast_to(cells_p[:, x : x + 1], (8, 128))
+    hot = jnp.concatenate(hots, axis=0)
+    onehot[...] = hot.astype(BF16)
+    hot = jnp.transpose(hot).astype(BF16)
+    onehot_t[...] = jnp.concatenate([hot, hot], axis=1)
     ins[2].wait()
 
     row16 = iota((16, 128), 0)
 
-    @pl.loop(0, groups)
-    def _(i):
-        vox = vol[pl.ds(i, 1), :]
-        parts = []
-        for k in range(8):
-            t = k // 2
-            spread = jnp.broadcast_to(vox[:, t * 128 : (t + 1) * 128], (16, 128))
-            parts.append(
-                jnp.where(row16 == k, spread, jnp.where(row16 == k + 8, 1.0, 0.0)).astype(BF16)
+    @pl.loop(0, groups // 2)
+    def _(pair):
+        both = []
+        for n, (begin, _) in enumerate(PIECES):
+
+            @pl.when(pair * 2 == begin)
+            def _(n=n):
+                load(n).wait()
+
+        for h in range(2):
+            i = pair * 2 + h
+            vox = vol[pl.ds(i, 1), :]
+            parts = []
+            for k in range(8):
+                t = k // 2
+                spread = jnp.broadcast_to(vox[:, t * 128 : (t + 1) * 128], (16, 128))
+                parts.append(
+                    jnp.where(row16 == k, spread, jnp.where(row16 == k + 8, 1.0, 0.0)).astype(BF16)
+                )
+            left = jnp.concatenate(parts, axis=1)
+            out = jnp.dot(left, wbuf[i], preferred_element_type=F32)
+            limit = den[pl.ds(pl.multiple_of(i * 8, 8), 8), :]
+            limit = jnp.concatenate([limit, limit], axis=1)
+            live = iota((8, 256), 1) < limit
+            both.append(
+                jnp.concatenate([jnp.where(live, out[0:8], 0.0), jnp.where(live, out[8:16], 0.0)], axis=1)
             )
-        left = jnp.concatenate(parts, axis=1)
-        load(i).wait()
-        out = jnp.dot(left, wbuf[i], preferred_element_type=F32)
-        at = pl.ds(pl.multiple_of(i * 8, 8), 8)
-        limit = den[at, :]
-        limit = jnp.concatenate([limit, limit], axis=1)
-        live = iota((8, 256), 1) < limit
-        contrib[at, 0:256] = jnp.where(live, out[0:8], 0.0)
-        contrib[at, 256:512] = jnp.where(live, out[8:16], 0.0)
-
-    hot = onehot[...].astype(BF16)
-    hot_t = jnp.transpose(onehot[...]).astype(BF16)
-    whole = contrib[...]
-    high = whole.astype(BF16)
-    low = (whole - high.astype(F32)).astype(BF16)
-    sums = jnp.dot(hot_t, high, preferred_element_type=F32) + jnp.dot(
-        hot_t, low, preferred_element_type=F32
-    )
+        whole = jnp.concatenate(both, axis=0)
+        high = whole.astype(BF16)
+        at = pl.multiple_of(pair * 16, 16)
+        contrib[pl.ds(at, 16), :] = high
+        contrib[pl.ds(at + 128, 16), :] = (whole - high.astype(F32)).astype(BF16)
+
+    sums = jnp.dot(onehot_t[...], contrib[...], preferred_element_type=F32)
     send_a[...] = sums.reshape(16, 8, 512)
 
-    pl.semaphore_wait(barrier, len(others))
+    pl.semaphore_wait(barrier, nx - 1 + jnp.where(s > 0, nx, 0) + jnp.where(s < ns - 1, nx, 0))
 
     def remote(src, dst, sem_send, sem_recv, ds, dr):
         return pltpu.make_async_remote_copy(
@@ -193,6 +198,25 @@
             device_id=(ds, dr), device_id_type=MESH,
         )
 
+    rounds = (ns - 2).bit_length()
+
+    def steps(k):
+        return [(s - (1 << k), s >= 1 << k), (s + (1 << k), s < ns - (1 << k))] if k < rounds else []
+
+    def tell(k):
+        for side, (there, ok) in enumerate(steps(k)):
+
+            @pl.when(ok)
+            def _():
+                pl.semaphore_signal(sem_k.at[2 * k + 1 - side], inc=1, device_id=(there, r), device_id_type=MESH)
+
+    def heard(k):
+        for side, (_, ok) in enumerate(steps(k)):
+
+            @pl.when(ok)
+            def _():
+                pl.semaphore_wait(sem_k.at[2 * k + side], 1)
+
     @pl.when(s > 0)
     def _():
         for g in range(2):
@@ -217,6 +241,7 @@
     sent(recv_a.at[pl.ds(0, nx - 1)], sem_s.at[0])
     sent(recv_a.at[pl.ds(0, 2)], sem_s.at[1], s > 0)
     sent(recv_a.at[pl.ds(0, 2)], sem_s.at[2], s < ns - 1)
+    tell(0)
     ins[3].wait()
     m = meas[...]
     seen = jnp.concatenate(
@@ -253,6 +278,8 @@
         rp = lax.rem(r + d, nx)
         remote(send_b, recv_b.at[2 + r], sem_s.at[3], sem_b.at[0], s, rp).start()
 
+    heard(0)
+    tell(1)
     sent(recv_b.at[pl.ds(0, nx - 1)], sem_s.at[3])
     sent(recv_b.at[pl.ds(0, nx)], sem_s.at[4], jnp.logical_or(low_edge, high_edge))
     for v in range(2):
@@ -274,8 +301,10 @@
     def _():
         remote(recv_b.at[pl.ds(10, 2)], recv_b.at[pl.ds(10, 2)], sem_s.at[3], sem_b.at[2], s, r).wait_recv()
 
+    heard(1)
+    tell(2)
     table = recv_b[...].astype(F32).reshape(128, 256).astype(BF16)
-    picked = jnp.dot(hot, table, preferred_element_type=F32)
+    picked = jnp.dot(onehot[...], table, preferred_element_type=F32)
     picked = jnp.where(live, picked, 0.0).reshape(16, 8, 256)
     lhs_b[...] = jnp.concatenate([picked, live3], axis=1).astype(BF16)
 
@@ -307,8 +336,6 @@
     cells3 = sart.reshape(2, 8, 512)
 
     ublk[...] = cells3
-    rows_lo[...] = cells3[:, 0:2, :]
-    rows_hi[...] = cells3[:, 6:8, :]
 
     def exists(ds, dr):
         ok = None
@@ -318,13 +345,13 @@
             ok = cond if ok is None else jnp.logical_and(ok, cond)
         return ok
 
-    def halo(n, ds, dr):
+    def edge(n, ds, dr):
         if dr == 0:
             src, dst = ublk, uside.at[1 if ds < 0 else 0]
         elif dr < 0:
-            src, dst = rows_lo, hnext.at[1 - ds]
+            src, dst = ublk.at[:, pl.ds(0, 2), :], halo.at[1 - ds, :, pl.ds(0, 2), :]
         else:
-            src, dst = rows_hi, hprev.at[1 - ds]
+            src, dst = ublk.at[:, pl.ds(6, 2), :], halo.at[1 - ds, :, pl.ds(6, 2), :]
         return remote(src, dst, sem_cs.at[n], sem_c.at[n], s + ds, r + dr)
 
     offsets = [(ds, dr) for ds in (-1, 1) for dr in (-1, 1, 0)] + [(0, -1), (0, 1)]
@@ -332,31 +359,32 @@
 
         @pl.when(exists(ds, dr))
         def _():
-            halo(n, ds, dr).start()
+            edge(n, ds, dr).start()
 
         pending.append(
-            lambda n=n, ds=ds, dr=dr: pl.when(exists(ds, dr))(lambda: halo(n, ds, dr).wait_send())
+            lambda n=n, ds=ds, dr=dr: pl.when(exists(ds, dr))(lambda: edge(n, ds, dr).wait_send())
         )
 
+    heard(2)
+    tell(3)
     for n, (ds, dr) in enumerate(offsets):
 
         @pl.when(exists(-ds, -dr))
         def _():
-            halo(n, ds, dr).wait_recv()
-
-    def padded(main, after, before):
-        return jnp.concatenate([main, after, jnp.zeros((4, 512), F32), before], axis=0)[None]
+            edge(n, ds, dr).wait_recv()
+
+    heard(3)
+    def padded(main, rim):
+        return jnp.concatenate([main, rim], axis=1)
 
     field = jnp.concatenate(
-        [padded(uside[0, p], hnext[0, p], hprev[0, p]) for p in range(2)]
-        + [padded(ublk[p], hnext[1, p], hprev[1, p]) for p in range(2)]
-        + [padded(uside[1, p], hnext[2, p], hprev[2, p]) for p in range(2)],
-        axis=0,
+        [padded(uside[0], halo[0]), padded(ublk[...], halo[1]), padded(uside[1], halo[2])], axis=0
     )
     slope = tv_slope(field)
 
     def reduce_all(n, parts):
         red_s[n] = parts
+        others = everyone_else(ns, nx, s, r)
         for j, (ds, dr) in enumerate(others):
             remote(red_s.at[n], red_in.at[n, j], sem_s.at[5 + n], sem_r.at[n], ds, dr).start()
         sent(red_in.at[n], sem_s.at[5 + n])
@@ -416,8 +444,9 @@
             pltpu.VMEM((2, 1024), F32),
             pltpu.VMEM((2, 8, 128), jnp.int32),
             pltpu.VMEM((2, 8, 128), jnp.int32),
-            pltpu.VMEM((128, 128), F32),
-            pltpu.VMEM((128, 512), F32),
+            pltpu.VMEM((128, 128), BF16),
+            pltpu.VMEM((128, 256), BF16),
+            pltpu.VMEM((256, 512), BF16),
             pltpu.VMEM((16, 8, 512), F32),
             pltpu.VMEM((2 * nx - 1, 8, 512), F32),
             pltpu.VMEM((8, 512), F32),
@@ -427,14 +456,11 @@
             pltpu.VMEM((32, 512), F32),
             pltpu.VMEM((128, 128), jnp.int32),
             pltpu.VMEM((2, 8, 512), F32),
-            pltpu.VMEM((2, 2, 512), F32),
-            pltpu.VMEM((2, 2, 512), F32),
             pltpu.VMEM((2, 2, 8, 512), F32),
-            pltpu.VMEM((3, 2, 2, 512), F32),
-            pltpu.VMEM((3, 2, 2, 512), F32),
+            pltpu.VMEM((3, 2, 8, 512), F32),
             pltpu.VMEM((2, 1, 128), F32),
             pltpu.VMEM((2, ns * nx - 1, 1, 128), F32),
-            dma((16,)),
+            dma((len(PIECES),)),
             dma((4,)),
             dma((7,)),
             dma((2,)),
@@ -442,6 +468,7 @@
             dma((8,)),
             dma((8,)),
             dma((2,)),
+            pltpu.SemaphoreType.REGULAR((8,)),
         ],
         compiler_params=pltpu.CompilerParams(
             collective_id=0, has_side_effects=True, vmem_limit_bytes=60 * 1024 * 1024

time: 40.2 us -> 39.4 us (0.980)
  Pallas kernels: 39.5 us -> 38.6 us
    pallas_call x1, Pallas kernels: 38.8 us -> 38 us  [body(): call(*[pltpu.with_memory_space_constraint(x, pltpu.HBM) for x in operands])]
where the time goes in v4:
time: 39.4 us; the launch traced here: 39.3 us
  Pallas kernels  38.6 us (98%)
  between operations  0.64 us (2%)
    pallas_call x1, Pallas kernels, body(): call(*[pltpu.with_memory_space_constraint(x, pltpu.HBM) for x in operands])  38 us

profile of v4, /device:TPU:1, one launch (start us, length us, event | category | flops | bytes accessed | tf_op | source)
XLA Modules:
  0.0 39.3 jit_solution(1922595483106907849)
XLA Ops:
  0.6 38.0 %shard_map.68 = (f32[2,8,512]{2,1,0:T(8,128)S(1)}, f32[2,1024]{1,0:T(2,128)S(1)}) custom-call(f32[16,512]{1,0:T(8,128)} %bitcast.5, bf16[16,1024,256]{2,1,0:T(8,128)(2,1)} %bitcast.4, s32[2,4,2,8]{3,2,1,0:T(2,128)} %bitcast.6, s32[2,4,2,8]{3,2,1,0:T(2,128)} %bitcast.7, f32[2,131072]{1,0:T(2,128)} %meas_hbm.1), custom_call_target="tpu_custom_call" | custom-call | tf_op jit(solution)/shard_map/pallas_call | solution.py:484
  38.6 0.6 %shard_map.69 = (f32[2,8,512]{2,1,0:T(8,128)}, f32[2,1024]{1,0:T(2,128)}) custom-call(f32[2,8,512]{2,1,0:T(8,128)S(1)} %get-tuple-element.4.upd, f32[2,1024]{1,0:T(2,128)S(1)} %get-tuple-element.5.cor), custom_call_target="tpu_custom_call" | custom-call | tf_op jit(solution)/shard_map/pallas_call | solution.py:485

commit v5 on v4

--- a/solution.py
+++ b/solution.py
@@ -74,7 +74,7 @@
     vol_hbm, foot_hbm, blk_hbm, cells_hbm, meas_hbm,
     upd_ref, cor_ref,
     vol, wbuf, blk, cells, meas, bcol, ccol, onehot, onehot_t, contrib,
-    send_a, recv_a, total, send_b, recv_b, lhs_b, num, den,
+    send_e, send_a, recv_a, total, send_b, recv_b, lhs_b, den,
     ublk, uside, halo,
     red_s, red_in,
     sem_w, sem_in, sem_s, sem_a, sem_b, sem_c, sem_cs, sem_r, sem_k,
@@ -85,11 +85,13 @@
     low_edge = jnp.logical_and(r < 2, s > 0)
     high_edge = jnp.logical_and(r >= nx - 2, s < ns - 1)
     pending = []
+    first = s % 2
 
     ins = [
         pltpu.make_async_copy(blk_hbm, blk, sem_in.at[0]),
         pltpu.make_async_copy(cells_hbm, cells, sem_in.at[1]),
-        pltpu.make_async_copy(vol_hbm, vol, sem_in.at[2]),
+        pltpu.make_async_copy(vol_hbm.at[first], vol.at[0], sem_in.at[2]),
+        pltpu.make_async_copy(vol_hbm.at[1 - first], vol.at[1], sem_in.at[4]),
         pltpu.make_async_copy(
             meas_hbm.at[:, pl.ds(pl.multiple_of((s * nx + r) * 1024, 1024), 1024)], meas, sem_in.at[3]
         ),
@@ -98,9 +100,11 @@
         c.start()
 
     def load(n):
-        first, last = PIECES[n]
-        at = pl.ds(first, last - first)
-        return pltpu.make_async_copy(foot_hbm.at[at], wbuf.at[at], sem_w.at[n])
+        begin, end = PIECES[n]
+        source = lax.rem(begin + first * 8, 16)
+        return pltpu.make_async_copy(
+            foot_hbm.at[pl.ds(source, end - begin)], wbuf.at[pl.ds(begin, end - begin)], sem_w.at[n]
+        )
 
     for n in range(len(PIECES)):
         load(n).start()
@@ -135,37 +139,36 @@
             ccol[p, 2 * t : 2 * t + 2, 0:8] = cells[p, t]
     lane = iota((8, 128), 1)
     view4 = (iota((8, 128), 0) & 1) * 4
-    first = (4 * s - 1) * 8
-    hots = []
-    for p in range(2):
-        blk_p = bcol[p]
-        cells_p = ccol[p]
+    lowest = (4 * s - 1) * 8
+    base = (1 - first) * 16
+    hots, near_hots = [], []
+    for q in range(2):
+        blk_p = bcol[(q + first) % 2]
+        cells_p = ccol[(q + first) % 2]
         for x in range(8):
-            i = p * 8 + x
-            near = jnp.broadcast_to(blk_p[:, x : x + 1], (8, 128)) - first
+            i = q * 8 + x
+            near = jnp.broadcast_to(blk_p[:, x : x + 1], (8, 128)) - lowest
             target = (near >> 2) * 8 + view4 + (near & 3)
             hots.append(jnp.where(lane == target, 1.0, 0.0))
+            if q == 1:
+                near_hots.append(jnp.where(lane == target - base, 1.0, 0.0))
             den[i * 8 : i * 8 + 8, :] = jnp.broadcast_to(cells_p[:, x : x + 1], (8, 128))
     hot = jnp.concatenate(hots, axis=0)
-    onehot[...] = hot.astype(BF16)
-    hot = jnp.transpose(hot).astype(BF16)
-    onehot_t[...] = jnp.concatenate([hot, hot], axis=1)
+    onehot[0:64, :] = hot[0:64].astype(BF16)
+    onehot[64:128, :] = jnp.concatenate(near_hots, axis=0).astype(BF16)
+    hot = jnp.transpose(hot)
+    for q in range(2):
+        part = hot[:, q * 64 : q * 64 + 64]
+        onehot_t[:, q * 128 : q * 128 + 128] = jnp.concatenate([part, part], axis=1).astype(BF16)
     ins[2].wait()
-
+    ins[3].wait()
     row16 = iota((16, 128), 0)
 
-    @pl.loop(0, groups // 2)
-    def _(pair):
+    def forward(slot, pair):
         both = []
-        for n, (begin, _) in enumerate(PIECES):
-
-            @pl.when(pair * 2 == begin)
-            def _(n=n):
-                load(n).wait()
-
         for h in range(2):
             i = pair * 2 + h
-            vox = vol[pl.ds(i, 1), :]
+            vox = vol[slot, pl.ds(i - slot * 8, 1), :]
             parts = []
             for k in range(8):
                 t = k // 2
@@ -183,12 +186,27 @@
             )
         whole = jnp.concatenate(both, axis=0)
         high = whole.astype(BF16)
-        at = pl.multiple_of(pair * 16, 16)
+        at = pl.multiple_of(pair * 16 + slot * 64, 16)
         contrib[pl.ds(at, 16), :] = high
-        contrib[pl.ds(at + 128, 16), :] = (whole - high.astype(F32)).astype(BF16)
-
-    sums = jnp.dot(onehot_t[...], contrib[...], preferred_element_type=F32)
-    send_a[...] = sums.reshape(16, 8, 512)
+        contrib[pl.ds(at + 64, 16), :] = (whole - high.astype(F32)).astype(BF16)
+
+    def forward_slot(slot):
+        @pl.loop(slot * 4, slot * 4 + 4)
+        def _(pair):
+            for n, (begin, _) in enumerate(PIECES):
+                if begin // 8 == slot:
+
+                    @pl.when(pair * 2 == begin)
+                    def _(n=n):
+                        load(n).wait()
+
+            forward(slot, pair)
+
+        k = slice(slot * 128, slot * 128 + 128)
+        sums = jnp.dot(onehot_t[:, k], contrib[k, :], preferred_element_type=F32)
+        return sums.reshape(16, 8, 512)
+
+    send_e[...] = forward_slot(0)
 
     pl.semaphore_wait(barrier, nx - 1 + jnp.where(s > 0, nx, 0) + jnp.where(s < ns - 1, nx, 0))
 
@@ -217,21 +235,33 @@
             def _():
                 pl.semaphore_wait(sem_k.at[2 * k + side], 1)
 
-    @pl.when(s > 0)
+    @pl.when(jnp.logical_and(first == 0, s > 0))
     def _():
         for g in range(2):
-            remote(send_a.at[g], recv_a.at[nx - 1 + r], sem_s.at[1], sem_a.at[1], s - 1, nx - 2 + g).start()
-
-    @pl.when(s < ns - 1)
+            remote(send_e.at[g], recv_a.at[nx - 1 + r], sem_s.at[1], sem_a.at[1], s - 1, nx - 2 + g).start()
+
+    @pl.when(jnp.logical_and(first == 1, s < ns - 1))
     def _():
         for g in range(2):
-            remote(send_a.at[10 + g], recv_a.at[nx - 1 + r], sem_s.at[2], sem_a.at[1], s + 1, g).start()
+            remote(send_e.at[10 + g], recv_a.at[nx - 1 + r], sem_s.at[2], sem_a.at[1], s + 1, g).start()
+
+    send_a[...] = send_e[...] + forward_slot(1)
 
     @pl.loop(1, nx)
     def _(d):
         rp = lax.rem(r + d, nx)
         remote(send_a.at[2 + rp], recv_a.at[d - 1], sem_s.at[0], sem_a.at[0], s, rp).start()
 
+    @pl.when(jnp.logical_and(first == 1, s > 0))
+    def _():
+        for g in range(2):
+            remote(send_a.at[g], recv_a.at[nx - 1 + r], sem_s.at[1], sem_a.at[1], s - 1, nx - 2 + g).start()
+
+    @pl.when(jnp.logical_and(first == 0, s < ns - 1))
+    def _():
+        for g in range(2):
+            remote(send_a.at[10 + g], recv_a.at[nx - 1 + r], sem_s.at[2], sem_a.at[1], s + 1, g).start()
+
     def sent(ref, sem, cond=None):
         def wait():
             remote(ref, ref, sem, sem_a.at[0], s, r).wait_send()
@@ -242,7 +272,7 @@
     sent(recv_a.at[pl.ds(0, 2)], sem_s.at[1], s > 0)
     sent(recv_a.at[pl.ds(0, 2)], sem_s.at[2], s < ns - 1)
     tell(0)
-    ins[3].wait()
+    ins[4].wait()
     m = meas[...]
     seen = jnp.concatenate(
         [m[v : v + 1, q * 256 : (q + 1) * 256] for v in range(2) for q in range(4)], axis=0
@@ -291,30 +321,23 @@
     live = iota((128, 256), 1) < limit
     live3 = jnp.where(live, 1.0, 0.0).reshape(16, 8, 256)
 
-    remote(recv_b.at[pl.ds(0, nx - 1)], recv_b.at[pl.ds(0, nx - 1)], sem_s.at[3], sem_b.at[0], s, r).wait_recv()
-
-    @pl.when(s > 0)
-    def _():
-        remote(recv_b.at[pl.ds(0, 2)], recv_b.at[pl.ds(0, 2)], sem_s.at[3], sem_b.at[1], s, r).wait_recv()
-
-    @pl.when(s < ns - 1)
-    def _():
-        remote(recv_b.at[pl.ds(10, 2)], recv_b.at[pl.ds(10, 2)], sem_s.at[3], sem_b.at[2], s, r).wait_recv()
-
-    heard(1)
-    tell(2)
-    table = recv_b[...].astype(F32).reshape(128, 256).astype(BF16)
-    picked = jnp.dot(onehot[...], table, preferred_element_type=F32)
-    picked = jnp.where(live, picked, 0.0).reshape(16, 8, 256)
-    lhs_b[...] = jnp.concatenate([picked, live3], axis=1).astype(BF16)
+    def arrived(sem, cond):
+        @pl.when(cond)
+        def _():
+            remote(recv_b.at[pl.ds(0, 2)], recv_b.at[pl.ds(0, 2)], sem_s.at[3], sem, s, r).wait_recv()
 
     row8 = iota((8, 128), 0)
 
-    @pl.loop(0, 2)
-    def _(p):
+    def back(slot, table):
+        half = slice(slot * 64, slot * 64 + 64)
+        table = table.astype(F32).reshape(table.shape[0] * 8, 256).astype(BF16)
+        hot = onehot[half, :]
+        found = jnp.dot(hot, table, preferred_element_type=F32)
+        found = jnp.where(live[half], found, 0.0).reshape(8, 8, 256)
+        lhs_b[slot * 8 : slot * 8 + 8] = jnp.concatenate([found, live3[slot * 8 : slot * 8 + 8]], axis=1).astype(BF16)
         tops, bottoms = [], []
         for x in range(8):
-            i = p * 8 + x
+            i = slot * 8 + x
             out = lax.dot_general(
                 lhs_b[i], wbuf[i], (((1,), (1,)), ((), ())), preferred_element_type=F32
             )
@@ -327,15 +350,23 @@
                     )
                     lanes.append(jnp.sum(both, axis=0, keepdims=True))
                 into.append(jnp.concatenate(lanes, axis=1))
-        num[pl.ds(pl.multiple_of(p * 8, 8), 8), :] = jnp.concatenate(tops, axis=0)
-        num[pl.ds(pl.multiple_of(p * 8 + 16, 8), 8), :] = jnp.concatenate(bottoms, axis=0)
-
-    before = vol[...]
-    sart = jnp.maximum(before + num[0:groups] / num[groups : 2 * groups], 0.0)
-    gap = (sart - before).reshape(2, 8, 512)
-    cells3 = sart.reshape(2, 8, 512)
-
-    ublk[...] = cells3
+        shift = jnp.concatenate(tops, axis=0) / jnp.concatenate(bottoms, axis=0)
+        sart = jnp.maximum(vol[slot] + shift, 0.0)
+        ublk[(slot + first) % 2] = sart
+        return sart - vol[slot]
+
+    remote(recv_b.at[pl.ds(0, nx - 1)], recv_b.at[pl.ds(0, nx - 1)], sem_s.at[3], sem_b.at[0], s, r).wait_recv()
+    arrived(sem_b.at[1], jnp.logical_and(first == 1, s > 0))
+    arrived(sem_b.at[2], jnp.logical_and(first == 0, s < ns - 1))
+    heard(1)
+    tell(2)
+    pad = jnp.zeros((6, 8, 256), BF16)
+    gap1 = back(1, jnp.concatenate([recv_b[pl.ds((1 - first) * 2, 10)], pad], axis=0))
+    arrived(sem_b.at[1], jnp.logical_and(first == 0, s > 0))
+    arrived(sem_b.at[2], jnp.logical_and(first == 1, s < ns - 1))
+    gap0 = back(0, recv_b[...])
+    gap = jnp.concatenate([gap0[None], gap1[None]], axis=0)
+
 
     def exists(ds, dr):
         ok = None
@@ -437,7 +468,7 @@
         in_specs=[any_space] * 5,
         out_specs=(vmem, vmem),
         scratch_shapes=[
-            pltpu.VMEM((16, 512), F32),
+            pltpu.VMEM((2, 8, 512), F32),
             pltpu.VMEM((16, 1024, 256), BF16),
             pltpu.VMEM((2, 4, 2, 8), jnp.int32),
             pltpu.VMEM((2, 4, 2, 8), jnp.int32),
@@ -448,12 +479,12 @@
             pltpu.VMEM((128, 256), BF16),
             pltpu.VMEM((256, 512), BF16),
             pltpu.VMEM((16, 8, 512), F32),
+            pltpu.VMEM((16, 8, 512), F32),
             pltpu.VMEM((2 * nx - 1, 8, 512), F32),
             pltpu.VMEM((8, 512), F32),
             pltpu.VMEM((8, 256), BF16),
             pltpu.VMEM((16, 8, 256), BF16),
             pltpu.VMEM((16, 16, 256), BF16),
-            pltpu.VMEM((32, 512), F32),
             pltpu.VMEM((128, 128), jnp.int32),
             pltpu.VMEM((2, 8, 512), F32),
             pltpu.VMEM((2, 2, 8, 512), F32),
@@ -461,7 +492,7 @@
             pltpu.VMEM((2, 1, 128), F32),
             pltpu.VMEM((2, ns * nx - 1, 1, 128), F32),
             dma((len(PIECES),)),
-            dma((4,)),
+            dma((5,)),
             dma((7,)),
             dma((2,)),
             dma((3,)),
@@ -475,7 +506,7 @@
         ),
     )
     operands = (
-        volume.reshape(16, 512),
+        volume,
         footprint.reshape(16, 1024, 256),
         jnp.transpose(tile_block, (0, 2, 3, 1)),
         jnp.transpose(tile_cells, (0, 2, 3, 1)),

time: 39.4 us -> 38.9 us (0.987)
  Pallas kernels: 38.6 us -> 38.1 us
    pallas_call x1, Pallas kernels: 38 us -> 37.5 us  [body(): call(*[pltpu.with_memory_space_constraint(x, pltpu.HBM) for x in operands])]
where the time goes in v5:
time: 38.9 us; the launch traced here: 38.8 us
  Pallas kernels  38.1 us (98%)
  between operations  0.64 us (2%)
    pallas_call x1, Pallas kernels, body(): call(*[pltpu.with_memory_space_constraint(x, pltpu.HBM) for x in operands])  37.5 us

profile of v5, /device:TPU:1, one launch (start us, length us, event | category | flops | bytes accessed | tf_op | source)
XLA Modules:
  0.0 38.8 jit_solution(12906295704960782130)
XLA Ops:
  0.6 37.5 %shard_map.68 = (f32[2,8,512]{2,1,0:T(8,128)S(1)}, f32[2,1024]{1,0:T(2,128)S(1)}) custom-call(f32[2,8,512]{2,1,0:T(8,128)} %vol_hbm.1, bf16[16,1024,256]{2,1,0:T(8,128)(2,1)} %bitcast.3, s32[2,4,2,8]{3,2,1,0:T(2,128)} %bitcast.4, s32[2,4,2,8]{3,2,1,0:T(2,128)} %bitcast.5, f32[2,131072]{1,0:T(2,128)} %meas_hbm.1), custom_call_target="tpu_custom_call" | custom-call | tf_op jit(solution)/shard_map/pallas_call | solution.py:515
  38.1 0.6 %shard_map.69 = (f32[2,8,512]{2,1,0:T(8,128)}, f32[2,1024]{1,0:T(2,128)}) custom-call(f32[2,8,512]{2,1,0:T(8,128)S(1)} %get-tuple-element.4.upd, f32[2,1024]{1,0:T(2,128)S(1)} %get-tuple-element.5.cor), custom_call_target="tpu_custom_call" | custom-call | tf_op jit(solution)/shard_map/pallas_call | solution.py:516

commit v6 on v5

--- a/solution.py
+++ b/solution.py
@@ -86,6 +86,7 @@
     high_edge = jnp.logical_and(r >= nx - 2, s < ns - 1)
     pending = []
     first = s % 2
+    slow_owner = jnp.logical_or(jnp.logical_and(first == 0, r < 2), jnp.logical_and(first == 1, r >= nx - 2))
 
     ins = [
         pltpu.make_async_copy(blk_hbm, blk, sem_in.at[0]),
@@ -116,6 +117,7 @@
 
     recv_b[...] = jnp.zeros(recv_b.shape, BF16)
     uside[...] = jnp.zeros(uside.shape, F32)
+    recv_a[0 : nx - 1] = jnp.zeros((nx - 1, 8, 512), F32)
     halo[...] = jnp.zeros(halo.shape, F32)
 
     @pl.when(s > 0)
@@ -140,7 +142,7 @@
     lane = iota((8, 128), 1)
     view4 = (iota((8, 128), 0) & 1) * 4
     lowest = (4 * s - 1) * 8
-    base = (1 - first) * 16
+    base = (1 - first) * 32
     hots, near_hots = [], []
     for q in range(2):
         blk_p = bcol[(q + first) % 2]
@@ -250,7 +252,14 @@
     @pl.loop(1, nx)
     def _(d):
         rp = lax.rem(r + d, nx)
-        remote(send_a.at[2 + rp], recv_a.at[d - 1], sem_s.at[0], sem_a.at[0], s, rp).start()
+        for v, ok in ((0, True), (1, jnp.where(rp % 2 == 0, r <= 4, r >= 3))):
+            at = pl.ds(4 * v, 4)
+
+            @pl.when(ok)
+            def _(v=v, at=at):
+                remote(
+                    send_a.at[2 + rp, at], recv_a.at[d - 1, at], sem_s.at[7 * v], sem_a.at[2 * v], s, rp
+                ).start()
 
     @pl.when(jnp.logical_and(first == 1, s > 0))
     def _():
@@ -268,7 +277,13 @@
 
         pending.append(wait if cond is None else lambda: pl.when(cond)(wait))
 
-    sent(recv_a.at[pl.ds(0, nx - 1)], sem_s.at[0])
+    sent(recv_a.at[pl.ds(0, nx - 1), pl.ds(0, 4)], sem_s.at[0])
+    middle = jnp.logical_or(r == 3, r == 4)
+    self_half = jnp.where(r % 2 == 0, r <= 4, r >= 3)
+    sent(recv_a.at[pl.ds(0, nx - 1), pl.ds(0, 4)], sem_s.at[7], middle)
+    outer = jnp.logical_not(middle)
+    sent(recv_a.at[pl.ds(0, 3), pl.ds(0, 4)], sem_s.at[7], jnp.logical_and(outer, self_half))
+    sent(recv_a.at[pl.ds(0, 4), pl.ds(0, 4)], sem_s.at[7], jnp.logical_and(outer, jnp.logical_not(self_half)))
     sent(recv_a.at[pl.ds(0, 2)], sem_s.at[1], s > 0)
     sent(recv_a.at[pl.ds(0, 2)], sem_s.at[2], s < ns - 1)
     tell(0)
@@ -278,7 +293,15 @@
         [m[v : v + 1, q * 256 : (q + 1) * 256] for v in range(2) for q in range(4)], axis=0
     )
     own = send_a[2 + r]
-    remote(send_a.at[pl.ds(0, nx - 1)], recv_a.at[pl.ds(0, nx - 1)], sem_s.at[0], sem_a.at[0], s, r).wait_recv()
+    part = recv_a.at[pl.ds(0, nx - 1), pl.ds(0, 4)]
+    remote(part, part, sem_s.at[0], sem_a.at[0], s, r).wait_recv()
+    for n, ok in ((4, self_half), (5, jnp.logical_not(self_half))):
+
+        @pl.when(ok)
+        def _(n=n):
+            part = recv_a.at[pl.ds(0, n), pl.ds(0, 4)]
+            remote(part, part, sem_s.at[0], sem_a.at[2], s, r).wait_recv()
+
     total[...] = own + jnp.sum(recv_a[0 : nx - 1], axis=0)
 
     @pl.when(jnp.logical_or(low_edge, high_edge))
@@ -306,7 +329,7 @@
     @pl.loop(1, nx)
     def _(d):
         rp = lax.rem(r + d, nx)
-        remote(send_b, recv_b.at[2 + r], sem_s.at[3], sem_b.at[0], s, rp).start()
+        remote(send_b, recv_b.at[2 + r], sem_s.at[3], sem_b.at[jnp.where(slow_owner, 3, 0)], s, rp).start()
 
     heard(0)
     tell(1)
@@ -321,11 +344,12 @@
     live = iota((128, 256), 1) < limit
     live3 = jnp.where(live, 1.0, 0.0).reshape(16, 8, 256)
 
-    def arrived(sem, cond):
+    def arrived(sem, cond, n=2):
         @pl.when(cond)
         def _():
-            remote(recv_b.at[pl.ds(0, 2)], recv_b.at[pl.ds(0, 2)], sem_s.at[3], sem, s, r).wait_recv()
-
+            remote(recv_b.at[pl.ds(0, n)], recv_b.at[pl.ds(0, n)], sem_s.at[3], sem, s, r).wait_recv()
+
+    other_owner = jnp.logical_not(slow_owner)
     row8 = iota((8, 128), 0)
 
     def back(slot, table):
@@ -355,15 +379,18 @@
         ublk[(slot + first) % 2] = sart
         return sart - vol[slot]
 
-    remote(recv_b.at[pl.ds(0, nx - 1)], recv_b.at[pl.ds(0, nx - 1)], sem_s.at[3], sem_b.at[0], s, r).wait_recv()
+    arrived(sem_b.at[0], slow_owner, nx - 2)
+    arrived(sem_b.at[0], other_owner, nx - 3)
     arrived(sem_b.at[1], jnp.logical_and(first == 1, s > 0))
     arrived(sem_b.at[2], jnp.logical_and(first == 0, s < ns - 1))
     heard(1)
     tell(2)
-    pad = jnp.zeros((6, 8, 256), BF16)
-    gap1 = back(1, jnp.concatenate([recv_b[pl.ds((1 - first) * 2, 10)], pad], axis=0))
+    pad = jnp.zeros((8, 8, 256), BF16)
+    gap1 = back(1, jnp.concatenate([recv_b[pl.ds((1 - first) * 4, 8)], pad], axis=0))
     arrived(sem_b.at[1], jnp.logical_and(first == 0, s > 0))
     arrived(sem_b.at[2], jnp.logical_and(first == 1, s < ns - 1))
+    arrived(sem_b.at[3], slow_owner, 1)
+    arrived(sem_b.at[3], other_owner)
     gap0 = back(0, recv_b[...])
     gap = jnp.concatenate([gap0[None], gap1[None]], axis=0)
 
@@ -420,7 +447,9 @@
             remote(red_s.at[n], red_in.at[n, j], sem_s.at[5 + n], sem_r.at[n], ds, dr).start()
         sent(red_in.at[n], sem_s.at[5 + n])
         remote(red_in.at[n], red_in.at[n], sem_s.at[5 + n], sem_r.at[n], s, r).wait_recv()
-        return parts + jnp.sum(red_in[n], axis=0)
+        even = len(others) // 8 * 8
+        sums = jnp.sum(red_in[n, 0:even].reshape(8, even // 8, 1, 128), axis=1)
+        return parts + jnp.sum(sums, axis=0) + jnp.sum(red_in[n, even:], axis=0)
 
     def half(x):
         return x + pltpu.roll(x, 64, 1)
@@ -493,9 +522,9 @@
             pltpu.VMEM((2, ns * nx - 1, 1, 128), F32),
             dma((len(PIECES),)),
             dma((5,)),
-            dma((7,)),
-            dma((2,)),
+            dma((8,)),
             dma((3,)),
+            dma((4,)),
             dma((8,)),
             dma((8,)),
             dma((2,)),

time: 38.9 us -> 38.7 us (level)
  no operation moved by 1% of the time
where the time goes in v6:
time: 38.7 us; the launch traced here: 38.6 us
  Pallas kernels  37.9 us (98%)
  between operations  0.64 us (2%)
    pallas_call x1, Pallas kernels, body(): call(*[pltpu.with_memory_space_constraint(x, pltpu.HBM) for x in operands])  37.3 us

profile of v6, /device:TPU:1, one launch (start us, length us, event | category | flops | bytes accessed | tf_op | source)
XLA Modules:
  0.0 38.6 jit_solution(329474816226378487)
XLA Ops:
  0.6 37.3 %shard_map.68 = (f32[2,8,512]{2,1,0:T(8,128)S(1)}, f32[2,1024]{1,0:T(2,128)S(1)}) custom-call(f32[2,8,512]{2,1,0:T(8,128)} %vol_hbm.1, bf16[16,1024,256]{2,1,0:T(8,128)(2,1)} %bitcast.3, s32[2,4,2,8]{3,2,1,0:T(2,128)} %bitcast.4, s32[2,4,2,8]{3,2,1,0:T(2,128)} %bitcast.5, f32[2,131072]{1,0:T(2,128)} %meas_hbm.1), custom_call_target="tpu_custom_call" | custom-call | tf_op jit(solution)/shard_map/pallas_call | solution.py:544
  37.9 0.6 %shard_map.69 = (f32[2,8,512]{2,1,0:T(8,128)}, f32[2,1024]{1,0:T(2,128)}) custom-call(f32[2,8,512]{2,1,0:T(8,128)S(1)} %get-tuple-element.4.upd, f32[2,1024]{1,0:T(2,128)S(1)} %get-tuple-element.5.cor), custom_call_target="tpu_custom_call" | custom-call | tf_op jit(solution)/shard_map/pallas_call | solution.py:545

commit v7 on v6

--- a/solution.py
+++ b/solution.py
@@ -108,7 +108,7 @@
         )
 
     for n in range(len(PIECES)):
-        load(n).start()
+        load(n).start(priority=n // 2)
 
     barrier = pltpu.get_barrier_semaphore()
 

time: 38.7 us -> 38.7 us (level)
  no operation moved by 1% of the time
where the time goes in v7:
time: 38.7 us; the launch traced here: 38.6 us
  Pallas kernels  37.9 us (98%)
  between operations  0.64 us (2%)
    pallas_call x1, Pallas kernels, body(): call(*[pltpu.with_memory_space_constraint(x, pltpu.HBM) for x in operands])  37.3 us

profile of v7, /device:TPU:1, one launch (start us, length us, event | category | flops | bytes accessed | tf_op | source)
XLA Modules:
  0.0 38.6 jit_solution(6215423687190267956)
XLA Ops:
  0.6 37.3 %shard_map.68 = (f32[2,8,512]{2,1,0:T(8,128)S(1)}, f32[2,1024]{1,0:T(2,128)S(1)}) custom-call(f32[2,8,512]{2,1,0:T(8,128)} %vol_hbm.1, bf16[16,1024,256]{2,1,0:T(8,128)(2,1)} %bitcast.3, s32[2,4,2,8]{3,2,1,0:T(2,128)} %bitcast.4, s32[2,4,2,8]{3,2,1,0:T(2,128)} %bitcast.5, f32[2,131072]{1,0:T(2,128)} %meas_hbm.1), custom_call_target="tpu_custom_call" | custom-call | tf_op jit(solution)/shard_map/pallas_call | solution.py:544
  37.9 0.6 %shard_map.69 = (f32[2,8,512]{2,1,0:T(8,128)}, f32[2,1024]{1,0:T(2,128)}) custom-call(f32[2,8,512]{2,1,0:T(8,128)S(1)} %get-tuple-element.4.upd, f32[2,1024]{1,0:T(2,128)S(1)} %get-tuple-element.5.cor), custom_call_target="tpu_custom_call" | custom-call | tf_op jit(solution)/shard_map/pallas_call | solution.py:545
